TPU v7x, 32 devices: a whole 2x2x4 slice. The times are simulated.
32 devices in a mesh: rows: 8 (over z, core), grp: 4 (over y, x).
Axes of the slice: x: 2, y: 2, z: 4, core: 2. Of those that a mesh axis runs over, the one named last changes fastest.
Arguments:
- sorted_rows: bfloat16 [8192, 2048], P(('rows', 'grp')), may hold values from -6 to 6
- combine: bfloat16 [8192], P(('rows', 'grp')), may hold values from 0.099609375 to 1
- cotangent: bfloat16 [8192, 2048], P(('rows', 'grp')), may hold values from -6 to 6
- starts: int32 [32], P(('rows', 'grp')), may hold values from 0 to 8191, as said below
- w_gate: bfloat16 [32, 2048, 768], P(('rows', 'grp')), may hold values from -0.125 to 0.125
- w_up: bfloat16 [32, 2048, 768], P(('rows', 'grp')), may hold values from -0.125 to 0.125
- w_down: bfloat16 [32, 768, 2048], P(('rows', 'grp')), may hold values from -0.21875 to 0.21875
Outputs:
- mixed: bfloat16 [8192, 2048], P(('rows', 'grp'))
- combine_grad: bfloat16 [8192], P(('rows', 'grp'))
- input_grad: bfloat16 [8192, 2048], P(('rows', 'grp'))
- grad_gate: bfloat16 [32, 2048, 768], P(('rows', 'grp'))
- grad_up: bfloat16 [32, 2048, 768], P(('rows', 'grp'))
- grad_down: bfloat16 [32, 768, 2048], P(('rows', 'grp'))
Inputs may be any that keep to these rules, and one draw needn't show every extreme that they name: starts[e] is the first sorted row of expert e; starts[0] = 0, starts[31] = 8191, and 256 * e < starts[e] < 256 * (e + 1) for e >= 1, so the rows of expert e lie in shards e and e + 1 of 256 rows, and every shard after the first begins with rows of the previous expert.
All inputs are finite; a program needn't handle non-finite values.
Results may differ from a plain program's by a relative error of at most 0.0058.
Values may be sent and summed in bfloat16 or wider, within the bound.
No kernel may reach another device: no remote copies, remote signals or barrier semaphores. Data moves between devices by JAX's collectives and lax.ppermute only.
A program may use at most 128 MiB of HBM per device.

v0:
```python
import jax
import jax.numpy as jnp
from jax import lax
from jax.sharding import PartitionSpec as P


def from_behind(block, axis, distance):
    devices = range(lax.axis_size(axis))
    route = [(i - distance, i) for i in devices if i - distance in devices]
    return lax.ppermute(block, axis, route)


def contract_rows(left, right):
    return lax.dot_general(
        left, right, (((0,), (0,)), ((), ())), preferred_element_type=jnp.float32
    )


def contract_cols(left, right):
    return lax.dot_general(
        left, right, (((1,), (1,)), ((), ())), preferred_element_type=jnp.float32
    )


def run_expert(rows_in, combine_rows, cotan_rows, keep, gate_w, up_w, down_w):
    gate_pre = jnp.dot(rows_in, gate_w, preferred_element_type=jnp.float32)
    up_pre = jnp.dot(rows_in, up_w, preferred_element_type=jnp.float32)
    sig_gate = jax.nn.sigmoid(gate_pre)
    silu_gate = gate_pre * sig_gate
    hidden = (silu_gate * up_pre).astype(jnp.bfloat16)
    expert_out = jnp.dot(hidden, down_w, preferred_element_type=jnp.float32)
    scale_col = combine_rows.astype(jnp.float32)[:, None]
    mixed = (scale_col * expert_out).astype(jnp.bfloat16)
    comb_grad = jnp.sum(expert_out * cotan_rows.astype(jnp.float32), axis=1).astype(jnp.bfloat16)
    out_grad = (scale_col * cotan_rows.astype(jnp.float32)).astype(jnp.bfloat16)
    out_grad = jnp.where(keep[:, None], out_grad, jnp.zeros_like(out_grad))
    hidden_grad = contract_cols(out_grad, down_w)
    gate_grad = (hidden_grad * up_pre * sig_gate * (1.0 + gate_pre * (1.0 - sig_gate))).astype(
        jnp.bfloat16
    )
    up_grad = (hidden_grad * silu_gate).astype(jnp.bfloat16)
    in_grad = (contract_cols(gate_grad, gate_w) + contract_cols(up_grad, up_w)).astype(jnp.bfloat16)
    gate_wgrad = contract_rows(rows_in, gate_grad)
    up_wgrad = contract_rows(rows_in, up_grad)
    down_wgrad = contract_rows(hidden, out_grad)
    return (mixed, comb_grad, in_grad, gate_wgrad, up_wgrad, down_wgrad)


def on_device(sorted_rows, combine, cotangent, starts, w_gate, w_up, w_down):
    count_rows = sorted_rows.shape[0]
    lead_count = jnp.remainder(starts[0], count_rows)
    lead_mask = jnp.arange(count_rows, dtype=jnp.int32) < lead_count
    own_mask = jnp.logical_not(lead_mask)
    zero_rows = jnp.zeros_like(sorted_rows)
    outgoing = (
        jnp.where(lead_mask[:, None], sorted_rows, zero_rows),
        jnp.where(lead_mask[:, None], cotangent, jnp.zeros_like(cotangent)),
        jnp.where(lead_mask, combine, jnp.zeros_like(combine)),
    )
    incoming = from_behind((outgoing[0], outgoing[1], outgoing[2]), ("rows", "grp"), -1)
    rows_all = jnp.concatenate([sorted_rows, incoming[0]], axis=0)
    cotan_all = jnp.concatenate([cotangent, incoming[1]], axis=0)
    comb_all = jnp.concatenate([combine, incoming[2]], axis=0)
    keep_all = jnp.concatenate([own_mask, jnp.ones((count_rows,), jnp.bool_)], axis=0)
    result = run_expert(rows_all, comb_all, cotan_all, keep_all, w_gate[0], w_up[0], w_down[0])
    back = from_behind(
        (result[0][count_rows:], result[1][count_rows:], result[2][count_rows:]), ("rows", "grp"), 1
    )
    mixed = jnp.where(lead_mask[:, None], back[0], result[0][:count_rows])
    comb_grad = jnp.where(lead_mask, back[1], result[1][:count_rows])
    in_grad = jnp.where(lead_mask[:, None], back[2], result[2][:count_rows])
    grad_gate = result[3][None].astype(jnp.bfloat16)
    grad_up = result[4][None].astype(jnp.bfloat16)
    grad_down = result[5][None].astype(jnp.bfloat16)
    return (mixed, comb_grad, in_grad, grad_gate, grad_up, grad_down)


def solution(mesh):
    in_specs = (
        P(("rows", "grp"), None),
        P(("rows", "grp")),
        P(("rows", "grp"), None),
        P(("rows", "grp")),
        P(("rows", "grp"), None, None),
        P(("rows", "grp"), None, None),
        P(("rows", "grp"), None, None),
    )
    out_specs = (
        P(("rows", "grp"), None),
        P(("rows", "grp")),
        P(("rows", "grp"), None),
        P(("rows", "grp"), None, None),
        P(("rows", "grp"), None, None),
        P(("rows", "grp"), None, None),
    )
    return jax.shard_map(
        on_device, mesh=mesh, in_specs=in_specs, out_specs=out_specs, check_vma=False
    )
```

profile of v0, /device:TPU:17, one launch (start us, length us, event | category | flops | bytes accessed | tf_op | source)
XLA Modules:
  0.0 117.5 jit_solution(17665191099015415402)
XLA Ops:
  0.6 0.0 copy-start
  1.5 0.0 copy-start.2
  1.5 0.0 copy-start.3
  1.5 2.3 %broadcast_select_fusion.1 = (bf16[256,2048]{1,0:T(8,128)(2,1)S(1)}, bf16[512,2048]{1,0:T(8,128)(2,1)S(1)}, bf16[256,2048]{1,0:T(8,128)(2,1)S(1)}) fusion(bf16[256,2048]{1,0:T(8,128)(2,1)} %param.7, pred[256]{0:T(512)(128)(4,1)S(1)} %iota_compare_fusion, bf16[256,2048]{1,0:T(8,128)(2,1)} %param.9), kind=kLoop, calls=%fused_computation.34 | loop fusion | flops 1048575 | bytes 5243136 | tf_op jit(solution)/shard_map/jit(_where)/select_n | solution.py:56
  3.8 4.6 %collective-permute-start.1 = (bf16[256,2048]{1,0:T(8,128)(2,1)S(1)}, bf16[256,2048]{1,0:T(8,128)(2,1)S(1)}, u32[]{:S(2)}, u32[]{:S(2)}) collective-permute-start(bf16[256,2048]{1,0:T(8,128)(2,1)S(1)} %get-tuple-element.11), channel_id=1, source_target_pairs={{1,0},{2,1},{3,2},{4,3},{5,4},{6,5},{7,6},{8,7},{9,8},{10,9},{11,1... | collective-permute-start | bytes 3145736 | tf_op jit(solution)/shard_map/ppermute | solution.py:10
  8.5 2.4 %collective-permute-start.3 = (bf16[256,2048]{1,0:T(8,128)(2,1)S(1)}, bf16[256,2048]{1,0:T(8,128)(2,1)S(1)}, u32[]{:S(2)}, u32[]{:S(2)}) collective-permute-start(bf16[256,2048]{1,0:T(8,128)(2,1)S(1)} %get-tuple-element.15), channel_id=1, source_target_pairs={{1,0},{2,1},{3,2},{4,3},{5,4},{6,5},{7,6},{8,7},{9,8},{10,9},{11,1... | collective-permute-start | bytes 3145736 | tf_op jit(solution)/shard_map/ppermute | solution.py:10
  10.9 0.0 copy-done.2
  11.0 3.3 %collective-permute-start = (bf16[256]{0:T(256)(128)(2,1)S(1)}, bf16[256]{0:T(256)(128)(2,1)S(1)}, u32[]{:S(2)}, u32[]{:S(2)}) collective-permute-start(bf16[256]{0:T(256)(128)(2,1)S(1)} %broadcast_select_fusion.2), channel_id=1, source_target_pairs={{1,0},{2,1},{3,2},{4,3},{5,4},{6,5},{7,6},{8,7},{9,8},{10,9},{11,1... | collective-permute-start | bytes 1544 | tf_op jit(solution)/shard_map/ppermute | solution.py:10
  14.3 39.6 %collective-permute-done = bf16[256]{0:T(256)(128)(2,1)S(1)} collective-permute-done((bf16[256]{0:T(256)(128)(2,1)S(1)}, bf16[256]{0:T(256)(128)(2,1)S(1)}, u32[]{:S(2)}, u32[]{:S(2)}) %collective-permute-start) | collective-permute-done | bytes 544 | tf_op jit(solution)/shard_map/ppermute | solution.py:10
  54.0 0.0 collective-permute-done.1
  54.0 0.1 constant_dynamic-update-slice_fusion
  54.0 0.0 copy-done.3
  54.1 0.0 copy-start.1
  54.1 0.0 copy-start.4
  54.1 1.8 %fusion.8 = f32[512,768]{1,0:T(8,128)S(1)} fusion(bf16[512,2048]{1,0:T(8,128)(2,1)S(1)} %constant_dynamic-update-slice_fusion, bf16[1,2048,768]{2,1,0:T(8,128)(2,1)S(1)} %copy-done.3), kind=kOutput, calls=%fused_computation.15 | convolution fusion | flops 1610612736 | bytes 6815744 | tf_op jit(solution)/shard_map/dot_general | solution.py:27
  55.9 0.0 collective-permute-done.3
  55.9 0.0 copy-done.1
  55.9 0.4 copy-done.4
  56.3 1.9 %fusion.2 = f32[512,768]{1,0:T(8,128)S(1)} fusion(bf16[1,768,2048]{2,1,0:T(8,128)(2,1)S(1)} %copy-done.4, f32[512]{0:T(512)S(1)} %maximum_convert_fusion, pred[512]{0:T(512)(128)(4,1)S(1)} %concatenate.19, bf16[256,2048]{1,0:T(8,128)(2,1)S(1)} %collective-permute-done.3, bf16[256,2048]{1,0:T(8,128)(2,1)S(1)} %copy-done.1), kind=kOutput, calls=%fused_computation.9 | convolution fusion | flops 1617952768 | bytes 6818304 | tf_op jit(solution)/shard_map/dot_general | solution.py:20
  58.1 0.0 copy-done
  58.1 2.4 %multiply_convert_fusion.2 = (bf16[512,768]{1,0:T(8,128)(2,1)S(1)}, bf16[512,768]{1,0:T(8,128)(2,1)S(1)}, bf16[512,768]{1,0:T(8,128)(2,1)S(1)}) fusion(f32[512,768]{1,0:T(8,128)S(1)} %fusion.2, f32[512,768]{1,0:T(8,128)S(1)} %fusion.8, bf16[512,2048]{1,0:T(8,128)(2,1)S(1)} %constant_dynamic-update-slice_fusion, bf16[1,2048,768]{2,1,0:T(8,128)(2,1)S(1)} %copy-done), kind=kOutput, calls=%fused_computation.27 | convolution fusion | flops 1616510976 | bytes 10747904 | tf_op jit(solution)/shard_map/dot_general | solution.py:26
  60.5 1.8 %fusion.6 = f32[512,2048]{1,0:T(8,128)S(1)} fusion(bf16[512,768]{1,0:T(8,128)(2,1)S(1)} %get-tuple-element.9, bf16[1,2048,768]{2,1,0:T(8,128)(2,1)S(1)} %copy-done.3), kind=kOutput, calls=%fused_computation.13 | convolution fusion | flops 1610612736 | bytes 8126464 | tf_op jit(solution)/shard_map/dot_general | solution.py:20
  62.4 1.8 %add_convert_fusion = bf16[512,2048]{1,0:T(8,128)(2,1)S(1)} fusion(f32[512,2048]{1,0:T(8,128)S(1)} %fusion.6, bf16[512,768]{1,0:T(8,128)(2,1)S(1)} %get-tuple-element.8, bf16[1,2048,768]{2,1,0:T(8,128)(2,1)S(1)} %copy-done), kind=kOutput, calls=%fused_computation.4 | convolution fusion | flops 1612709888 | bytes 10223616 | tf_op jit(solution)/shard_map/dot_general | solution.py:20
  64.2 0.1 slice.26
  64.3 2.3 %collective-permute-start.5 = (bf16[256,2048]{1,0:T(8,128)(2,1)S(1)}, bf16[256,2048]{1,0:T(8,128)(2,1)S(1)}, u32[]{:S(2)}, u32[]{:S(2)}) collective-permute-start(bf16[256,2048]{1,0:T(8,128)(2,1)S(1)} %slice.26), channel_id=1, source_target_pairs={{0,1},{1,2},{2,3},{3,4},{4,5},{5,6},{6,7},{7,8},{8,9},{9,10},{10,1... | collective-permute-start | bytes 3145736 | tf_op jit(solution)/shard_map/ppermute | solution.py:10
  66.6 2.1 %fusion = (bf16[512]{0:T(512)(128)(2,1)S(1)}, bf16[512,2048]{1,0:T(8,128)(2,1)S(1)}) fusion(bf16[256,2048]{1,0:T(8,128)(2,1)S(1)} %collective-permute-done.3, bf16[256,2048]{1,0:T(8,128)(2,1)S(1)} %copy-done.1, f32[512]{0:T(512)S(1)} %maximum_convert_fusion, bf16[512,768]{1,0:T(8,128)(2,1)S(1)} %get-tuple-element.10, bf16[1,768,2048]{2,1,0:T(8,128)(2,1)S(1)} %copy-done.4), kind=kOutput, calls=%fused_computation.2 | convolution fusion | flops 1619000832 | bytes 8129536 | tf_op jit(solution)/shard_map/dot_general | solution.py:31
  68.7 0.1 slice.24
  68.8 2.2 %collective-permute-start.2 = (bf16[256,2048]{1,0:T(8,128)(2,1)S(1)}, bf16[256,2048]{1,0:T(8,128)(2,1)S(1)}, u32[]{:S(2)}, u32[]{:S(2)}) collective-permute-start(bf16[256,2048]{1,0:T(8,128)(2,1)S(1)} %slice.24), channel_id=1, source_target_pairs={{0,1},{1,2},{2,3},{3,4},{4,5},{5,6},{6,7},{7,8},{8,9},{9,10},{10,1... | collective-permute-start | bytes 3145736 | tf_op jit(solution)/shard_map/ppermute | solution.py:10
  71.1 2.1 %collective-permute-start.4 = (bf16[256]{0:T(256)(128)(2,1)S(1)}, bf16[256]{0:T(256)(128)(2,1)S(1)}, u32[]{:S(2)}, u32[]{:S(2)}) collective-permute-start(bf16[256]{0:T(256)(128)(2,1)S(1)} %slice.20), channel_id=1, source_target_pairs={{0,1},{1,2},{2,3},{3,4},{4,5},{5,6},{6,7},{7,8},{8,9},{9,10},{10,1... | collective-permute-start | bytes 1544 | tf_op jit(solution)/shard_map/ppermute | solution.py:10
  73.2 3.6 %fusion.16 = bf16[1,768,2048]{2,1,0:T(8,128)(2,1)} fusion(bf16[512,768]{1,0:T(8,128)(2,1)S(1)} %get-tuple-element.10, f32[512]{0:T(512)S(1)} %maximum_convert_fusion, pred[512]{0:T(512)(128)(4,1)S(1)} %concatenate.19, bf16[256,2048]{1,0:T(8,128)(2,1)S(1)} %collective-permute-done.3, bf16[256,2048]{1,0:T(8,128)(2,1)S(1)} %copy-done.1), kind=kOutput, calls=%fused_computation.23 | convolution fusion | flops 1619525632 | bytes 6031872 | tf_op jit(solution)/shard_map/dot_general | solution.py:14
  76.8 3.5 %fusion.14 = bf16[1,2048,768]{2,1,0:T(8,128)(2,1)} fusion(bf16[512,2048]{1,0:T(8,128)(2,1)S(1)} %constant_dynamic-update-slice_fusion, bf16[512,768]{1,0:T(8,128)(2,1)S(1)} %get-tuple-element.8), kind=kOutput, calls=%fused_computation.21 | convolution fusion | flops 1612185600 | bytes 6029312 | tf_op jit(solution)/shard_map/dot_general | solution.py:14
  80.4 3.5 %fusion.15 = bf16[1,2048,768]{2,1,0:T(8,128)(2,1)} fusion(bf16[512,2048]{1,0:T(8,128)(2,1)S(1)} %constant_dynamic-update-slice_fusion, bf16[512,768]{1,0:T(8,128)(2,1)S(1)} %get-tuple-element.9), kind=kOutput, calls=%fused_computation.22 | convolution fusion | flops 1612185600 | bytes 6029312 | tf_op jit(solution)/shard_map/dot_general | solution.py:14
  83.9 31.3 %collective-permute-done.4 = bf16[256]{0:T(256)(128)(2,1)S(1)} collective-permute-done((bf16[256]{0:T(256)(128)(2,1)S(1)}, bf16[256]{0:T(256)(128)(2,1)S(1)}, u32[]{:S(2)}, u32[]{:S(2)}) %collective-permute-start.4) | collective-permute-done | bytes 544 | tf_op jit(solution)/shard_map/ppermute | solution.py:10
  115.2 0.5 slice_select_fusion.2
  115.7 0.0 collective-permute-done.5
  115.7 0.0 collective-permute-done.2
  115.7 1.7 %slice_select_fusion = (bf16[256,2048]{1,0:T(8,128)(2,1)}, bf16[256,2048]{1,0:T(8,128)(2,1)}) fusion(bf16[256,2048]{1,0:T(8,128)(2,1)S(1)} %collective-permute-done.5, bf16[512,2048]{1,0:T(8,128)(2,1)S(1)} %add_convert_fusion, pred[256]{0:T(512)(128)(4,1)S(1)} %iota_compare_fusion, bf16[256,2048]{1,0:T(8,128)(2,1)S(1)} %collective-permute-done.2, ...), kind=kLoop, calls=%fused_computation.31 | loop fusion | flops 1048576 | bytes 6291712 | tf_op jit(solution)/shard_map/jit(_where)/select_n | solution.py:71
  (6 shorter events, 0.0 us)
Async XLA Ops:
  0.6 57.5 %copy-start = (bf16[1,2048,768]{2,1,0:T(8,128)(2,1)S(1)}, bf16[1,2048,768]{2,1,0:T(8,128)(2,1)}, u32[]{:S(2)}) copy-start(bf16[1,2048,768]{2,1,0:T(8,128)(2,1)} %param.11) | copy-start | bytes 9437188
  1.5 9.5 %copy-start.2 = (bf16[256]{0:T(256)(128)(2,1)S(1)}, bf16[256]{0:T(256)(128)(2,1)}, u32[]{:S(2)}) copy-start(bf16[256]{0:T(256)(128)(2,1)} %param.8) | copy-start | bytes 1540
  1.5 52.6 %copy-start.3 = (bf16[1,2048,768]{2,1,0:T(8,128)(2,1)S(1)}, bf16[1,2048,768]{2,1,0:T(8,128)(2,1)}, u32[]{:S(2)}) copy-start(bf16[1,2048,768]{2,1,0:T(8,128)(2,1)} %param.12) | copy-start | bytes 9437188
  3.8 50.1 %collective-permute-start.1 = (bf16[256,2048]{1,0:T(8,128)(2,1)S(1)}, bf16[256,2048]{1,0:T(8,128)(2,1)S(1)}, u32[]{:S(2)}, u32[]{:S(2)}) collective-permute-start(bf16[256,2048]{1,0:T(8,128)(2,1)S(1)} %get-tuple-element.11), channel_id=1, source_target_pairs={{1,0},{2,1},{3,2},{4,3},{5,4},{6,5},{7,6},{8,7},{9,8},{10,9},{11,1... | collective-permute-start | bytes 3145736 | tf_op jit(solution)/shard_map/ppermute | solution.py:10
  8.5 47.4 %collective-permute-start.3 = (bf16[256,2048]{1,0:T(8,128)(2,1)S(1)}, bf16[256,2048]{1,0:T(8,128)(2,1)S(1)}, u32[]{:S(2)}, u32[]{:S(2)}) collective-permute-start(bf16[256,2048]{1,0:T(8,128)(2,1)S(1)} %get-tuple-element.15), channel_id=1, source_target_pairs={{1,0},{2,1},{3,2},{4,3},{5,4},{6,5},{7,6},{8,7},{9,8},{10,9},{11,1... | collective-permute-start | bytes 3145736 | tf_op jit(solution)/shard_map/ppermute | solution.py:10
  11.0 43.0 %collective-permute-start = (bf16[256]{0:T(256)(128)(2,1)S(1)}, bf16[256]{0:T(256)(128)(2,1)S(1)}, u32[]{:S(2)}, u32[]{:S(2)}) collective-permute-start(bf16[256]{0:T(256)(128)(2,1)S(1)} %broadcast_select_fusion.2), channel_id=1, source_target_pairs={{1,0},{2,1},{3,2},{4,3},{5,4},{6,5},{7,6},{8,7},{9,8},{10,9},{11,1... | collective-permute-start | bytes 1544 | tf_op jit(solution)/shard_map/ppermute | solution.py:10
  54.1 1.8 %copy-start.1 = (bf16[256,2048]{1,0:T(8,128)(2,1)S(1)}, bf16[256,2048]{1,0:T(8,128)(2,1)}, u32[]{:S(2)}) copy-start(bf16[256,2048]{1,0:T(8,128)(2,1)} %param.9) | copy-start | bytes 3145732
  54.1 2.2 %copy-start.4 = (bf16[1,768,2048]{2,1,0:T(8,128)(2,1)S(1)}, bf16[1,768,2048]{2,1,0:T(8,128)(2,1)}, u32[]{:S(2)}) copy-start(bf16[1,768,2048]{2,1,0:T(8,128)(2,1)} %param.13) | copy-start | bytes 9437188
  64.3 51.5 %collective-permute-start.5 = (bf16[256,2048]{1,0:T(8,128)(2,1)S(1)}, bf16[256,2048]{1,0:T(8,128)(2,1)S(1)}, u32[]{:S(2)}, u32[]{:S(2)}) collective-permute-start(bf16[256,2048]{1,0:T(8,128)(2,1)S(1)} %slice.26), channel_id=1, source_target_pairs={{0,1},{1,2},{2,3},{3,4},{4,5},{5,6},{6,7},{7,8},{8,9},{9,10},{10,1... | collective-permute-start | bytes 3145736 | tf_op jit(solution)/shard_map/ppermute | solution.py:10
  68.8 46.9 %collective-permute-start.2 = (bf16[256,2048]{1,0:T(8,128)(2,1)S(1)}, bf16[256,2048]{1,0:T(8,128)(2,1)S(1)}, u32[]{:S(2)}, u32[]{:S(2)}) collective-permute-start(bf16[256,2048]{1,0:T(8,128)(2,1)S(1)} %slice.24), channel_id=1, source_target_pairs={{0,1},{1,2},{2,3},{3,4},{4,5},{5,6},{6,7},{7,8},{8,9},{9,10},{10,1... | collective-permute-start | bytes 3145736 | tf_op jit(solution)/shard_map/ppermute | solution.py:10
  71.1 44.2 %collective-permute-start.4 = (bf16[256]{0:T(256)(128)(2,1)S(1)}, bf16[256]{0:T(256)(128)(2,1)S(1)}, u32[]{:S(2)}, u32[]{:S(2)}) collective-permute-start(bf16[256]{0:T(256)(128)(2,1)S(1)} %slice.20), channel_id=1, source_target_pairs={{0,1},{1,2},{2,3},{3,4},{4,5},{5,6},{6,7},{7,8},{8,9},{9,10},{10,1... | collective-permute-start | bytes 1544 | tf_op jit(solution)/shard_map/ppermute | solution.py:10
where the time goes:
time: 118 us; the launch traced here: 117 us
  waiting for transfers between devices  71 us (60%)
  matrix products  22.6 us (19%)
  starting transfers between devices  17.1 us (14%)
  other arithmetic  4.59 us (4%)
  between operations  1.67 us (1%)
    ppermute x6, waiting for transfers between devices, from_behind(): return lax.ppermute(block, axis, route)  71 us
    ppermute x6, starting transfers between devices, from_behind(): return lax.ppermute(block, axis, route)  17.1 us
    dot_general x3, matrix products, contract_rows(): lax.dot_general(left, right, (((0,), (0,)), ((), ())), preferred_element_...  10.7 us
    dot_general x3, matrix products, contract_cols(): lax.dot_general(left, right, (((1,), (1,)), ((), ())), preferred_element_...  5.53 us
    dot_general x1, matrix products, run_expert(): gate_pre = jnp.dot(rows_in, gate_w, preferred_element_type=jnp.float32)  2.37 us
  transfers between devices with their start and end apart: 6, of which 2 were waited for; matrix products, arithmetic and copies ran while one was open for 13% of the time, Pallas kernels for 0%

commit v1 on v0

v1 whole, which is shorter than its diff:
```python
import jax
import jax.numpy as jnp
from jax import lax
from jax.sharding import PartitionSpec as P


def from_behind(block, axis, distance):
    devices = range(lax.axis_size(axis))
    route = [(i - distance, i) for i in devices if i - distance in devices]
    return lax.ppermute(block, axis, route)


def contract_rows(left, right):
    return lax.dot_general(
        left, right, (((0,), (0,)), ((), ())), preferred_element_type=jnp.float32
    )


def contract_cols(left, right):
    return lax.dot_general(
        left, right, (((1,), (1,)), ((), ())), preferred_element_type=jnp.float32
    )


def expert_up(rows_in, gate_w, up_w):
    gate_pre = jnp.dot(rows_in, gate_w, preferred_element_type=jnp.float32)
    up_pre = jnp.dot(rows_in, up_w, preferred_element_type=jnp.float32)
    hidden = (gate_pre * jax.nn.sigmoid(gate_pre) * up_pre).astype(jnp.bfloat16)
    return lax.optimization_barrier((gate_pre, up_pre, hidden))


def expert_down(hidden, scale_col, down_w):
    expert_out = jnp.dot(hidden, down_w, preferred_element_type=jnp.float32)
    mixed = (scale_col * expert_out).astype(jnp.bfloat16)
    return lax.optimization_barrier((expert_out, mixed))


def output_grad(expert_out, scale_col, cotan_rows, keep):
    cotan_wide = cotan_rows.astype(jnp.float32)
    comb_grad = jnp.sum(expert_out * cotan_wide, axis=1).astype(jnp.bfloat16)
    out_grad = (scale_col * cotan_wide).astype(jnp.bfloat16)
    if keep is not None:
        out_grad = jnp.where(keep[:, None], out_grad, jnp.zeros_like(out_grad))
    return comb_grad, out_grad


def expert_back(out_grad, pre, gate_w, up_w, down_w):
    gate_pre, up_pre, _ = pre
    sig_gate = jax.nn.sigmoid(gate_pre)
    silu_gate = gate_pre * sig_gate
    hidden_grad = contract_cols(out_grad, down_w)
    gate_grad = (hidden_grad * up_pre * sig_gate * (1.0 + gate_pre * (1.0 - sig_gate))).astype(
        jnp.bfloat16
    )
    up_grad = (hidden_grad * silu_gate).astype(jnp.bfloat16)
    in_grad = (contract_cols(gate_grad, gate_w) + contract_cols(up_grad, up_w)).astype(jnp.bfloat16)
    return lax.optimization_barrier((gate_grad, up_grad, in_grad))


def device_step(sorted_rows, combine, cotangent, starts, w_gate, w_up, w_down):
    axes = ("rows", "grp")
    gate_w, up_w, down_w = w_gate[0], w_up[0], w_down[0]
    count_rows = sorted_rows.shape[0]
    lead_count = jnp.remainder(starts[0], count_rows)
    lead_mask = jnp.arange(count_rows, dtype=jnp.int32) < lead_count
    own_mask = jnp.logical_not(lead_mask)

    next_rows = from_behind(sorted_rows, axes, -1)
    next_comb = from_behind(jnp.where(lead_mask, combine, jnp.zeros_like(combine)), axes, -1)
    next_cotan = from_behind(cotangent, axes, -1)

    own_scale = combine.astype(jnp.float32)[:, None]
    own_pre = expert_up(sorted_rows, gate_w, up_w)
    own_out, own_mixed = expert_down(own_pre[2], own_scale, down_w)
    own_comb_grad, own_out_grad = output_grad(own_out, own_scale, cotangent, own_mask)
    own_gate_grad, own_up_grad, own_in_grad = expert_back(
        own_out_grad, own_pre, gate_w, up_w, down_w
    )

    next_scale = next_comb.astype(jnp.float32)[:, None]
    next_pre = expert_up(next_rows, gate_w, up_w)
    next_out, next_mixed = expert_down(next_pre[2], next_scale, down_w)
    back_mixed = from_behind(next_mixed, axes, 1)

    next_comb_grad, next_out_grad = output_grad(next_out, next_scale, next_cotan, None)
    next_gate_grad, next_up_grad, next_in_grad = expert_back(
        next_out_grad, next_pre, gate_w, up_w, down_w
    )
    back_comb_grad = from_behind(next_comb_grad, axes, 1)
    back_in_grad = from_behind(next_in_grad, axes, 1)

    rows_all = jnp.concatenate([sorted_rows, next_rows], axis=0)
    hidden_all = jnp.concatenate([own_pre[2], next_pre[2]], axis=0)
    out_grad_all = jnp.concatenate([own_out_grad, next_out_grad], axis=0)
    gate_grad_all = jnp.concatenate([own_gate_grad, next_gate_grad], axis=0)
    up_grad_all = jnp.concatenate([own_up_grad, next_up_grad], axis=0)
    grad_gate = contract_rows(rows_all, gate_grad_all)[None].astype(jnp.bfloat16)
    grad_up = contract_rows(rows_all, up_grad_all)[None].astype(jnp.bfloat16)
    grad_down = contract_rows(hidden_all, out_grad_all)[None].astype(jnp.bfloat16)

    mixed = jnp.where(lead_mask[:, None], back_mixed, own_mixed)
    comb_grad = jnp.where(lead_mask, back_comb_grad, own_comb_grad)
    in_grad = jnp.where(lead_mask[:, None], back_in_grad, own_in_grad)
    return (mixed, comb_grad, in_grad, grad_gate, grad_up, grad_down)


def solution(mesh):
    in_specs = (
        P(("rows", "grp"), None),
        P(("rows", "grp")),
        P(("rows", "grp"), None),
        P(("rows", "grp")),
        P(("rows", "grp"), None, None),
        P(("rows", "grp"), None, None),
        P(("rows", "grp"), None, None),
    )
    out_specs = (
        P(("rows", "grp"), None),
        P(("rows", "grp")),
        P(("rows", "grp"), None),
        P(("rows", "grp"), None, None),
        P(("rows", "grp"), None, None),
        P(("rows", "grp"), None, None),
    )
    return jax.shard_map(
        device_step, mesh=mesh, in_specs=in_specs, out_specs=out_specs, check_vma=False
    )
```

time: 118 us -> 115 us (0.975)
  waiting for transfers between devices: 71 us -> 64.3 us
  matrix products: 22.6 us -> 25.4 us
  local copies, waits for them, and re-layouts: 0.63 us -> 2.55 us
    ppermute x6, waiting for transfers between devices: 71 us -> 64.3 us  [from_behind(): return lax.ppermute(block, axis, route)]
    select_n x4 -> x3, other arithmetic: 4.57 us -> 2.4 us  [the longest x1 1.58 us: device_step(): in_grad = jnp.where(lead_mask[:, None], back_in_grad, own_in_grad)]
    unnamed x10 -> x11, local copies, waits for them, and re-layouts: 0.41 us -> 2.45 us
    dot_general x3 -> x6, matrix products: 6.29 us -> 8.08 us  [the longest x2 4.01 us: expert_up(): gate_pre = jnp.dot(rows_in, gate_w, preferred_element_type=jnp.float32)]
    convert_element_type x1 -> x3, other arithmetic: 0.01 us -> 1.36 us  [the longest x1 0.83 us: device_step(): own_scale = combine.astype(jnp.float32)[:, None]]
    dot_general x3 -> x6, matrix products: 5.53 us -> 6.73 us  [contract_cols(): lax.dot_general(left, right, (((1,), (1,)), ((), ())), preferred_element_...]
  transfers between devices with their start and end apart: 6 -> 6, of which waited for: 2 -> 3; matrix products, arithmetic and copies ran while one was open for 13% -> 24% of each run, Pallas kernels for 0% -> 0%
where the time goes in v1:
time: 115 us; the launch traced here: 114 us
  waiting for transfers between devices  64.3 us (56%)
  matrix products  25.4 us (22%)
  starting transfers between devices  16.4 us (14%)
  other arithmetic  4.07 us (4%)
  local copies, waits for them, and re-layouts  2.55 us (2%)
  between operations  1.72 us (1%)
    ppermute x6, waiting for transfers between devices, from_behind(): return lax.ppermute(block, axis, route)  64.3 us
    ppermute x6, starting transfers between devices, from_behind(): return lax.ppermute(block, axis, route)  16.4 us
    dot_general x3, matrix products, contract_rows(): lax.dot_general(left, right, (((0,), (0,)), ((), ())), preferred_element_...  10.6 us
    dot_general x6, matrix products, contract_cols(): lax.dot_general(left, right, (((1,), (1,)), ((), ())), preferred_element_...  6.73 us
    dot_general x2, matrix products, expert_up(): gate_pre = jnp.dot(rows_in, gate_w, preferred_element_type=jnp.float32)  4.01 us
    unnamed x11, local copies, waits for them, and re-layouts  2.45 us
  transfers between devices with their start and end apart: 6, of which 3 were waited for; matrix products, arithmetic and copies ran while one was open for 24% of the time, Pallas kernels for 0%

profile of v1, /device:TPU:17, one launch (start us, length us, event | category | flops | bytes accessed | tf_op | source)
XLA Modules:
  0.0 114.3 jit_solution(1568351917886874423)
XLA Ops:
  0.6 0.0 copy-start
  1.5 0.0 copy-start.4
  1.5 0.8 fusion.60
  2.3 4.6 %collective-permute-start.1 = (bf16[256]{0:T(256)(128)(2,1)S(1)}, bf16[256]{0:T(256)(128)(2,1)S(1)}, u32[]{:S(2)}, u32[]{:S(2)}) collective-permute-start(bf16[256]{0:T(256)(128)(2,1)S(1)} %get-tuple-element.47), channel_id=1, source_target_pairs={{1,0},{2,1},{3,2},{4,3},{5,4},{6,5},{7,6},{8,7},{9,8},{10,9},{11,1... | collective-permute-start | bytes 1544 | tf_op jit(solution)/shard_map/ppermute | solution.py:10
  6.9 2.4 %collective-permute-start.3 = (bf16[256,2048]{1,0:T(8,128)(2,1)}, bf16[256,2048]{1,0:T(8,128)(2,1)S(1)}, u32[]{:S(2)}, u32[]{:S(2)}) collective-permute-start(bf16[256,2048]{1,0:T(8,128)(2,1)} %param.9), channel_id=1, source_target_pairs={{1,0},{2,1},{3,2},{4,3},{5,4},{6,5},{7,6},{8,7},{9,8},{10,9},{11,1... | collective-permute-start | bytes 3145736 | tf_op jit(solution)/shard_map/ppermute | solution.py:10
  9.4 3.3 %collective-permute-start = (bf16[256,2048]{1,0:T(8,128)(2,1)}, bf16[256,2048]{1,0:T(8,128)(2,1)S(1)}, u32[]{:S(2)}, u32[]{:S(2)}) collective-permute-start(bf16[256,2048]{1,0:T(8,128)(2,1)} %param.7), channel_id=1, source_target_pairs={{1,0},{2,1},{3,2},{4,3},{5,4},{6,5},{7,6},{8,7},{9,8},{10,9},{11,1... | collective-permute-start | bytes 3145736 | tf_op jit(solution)/shard_map/ppermute | solution.py:10
  12.7 1.4 %constant_dynamic-update-slice_fusion.1 = bf16[512,2048]{1,0:T(8,128)(2,1)S(1)} fusion(bf16[256,2048]{1,0:T(8,128)(2,1)} %param.7), kind=kLoop, calls=%fused_computation.68 | loop fusion | bytes 2097152
  14.1 0.0 copy-done.4
  14.1 0.0 copy-start.2
  14.1 3.0 %fusion.20 = f32[256,768]{1,0:T(8,128)S(1)} fusion(bf16[256,2048]{1,0:T(8,128)(2,1)S(1)} %copy-done.4, bf16[1,2048,768]{2,1,0:T(8,128)(2,1)} %param.11), kind=kOutput, calls=%fused_computation.23 | convolution fusion | flops 805306368 | bytes 4980736 | tf_op jit(solution)/shard_map/dot_general | solution.py:26
  17.2 0.0 copy-done.2
  17.2 0.0 copy-start.3
  17.2 1.0 multiply_convert_fusion.6
  18.2 0.2 copy-done.3
  18.4 0.3 fusion.46
  18.7 0.0 copy-done
  18.7 1.0 multiply_convert_fusion
  19.8 1.4 %multiply_convert_fusion.2 = (bf16[256,768]{1,0:T(8,128)(2,1)S(1)}, bf16[256,768]{1,0:T(8,128)(2,1)S(1)}) fusion(f32[256,768]{1,0:T(8,128)S(1)} %fusion.20, f32[256,768]{1,0:T(8,128)S(1)} %get-tuple-element.31, bf16[256,2048]{1,0:T(8,128)(2,1)S(1)} %fusion.46, bf16[1,768,2048]{2,1,0:T(8,128)(2,1)S(1)} %copy-done), kind=kOutput, calls=%fused_computation.59 | convolution fusion | flops 807862272 | bytes 6553600 | tf_op jit(solution)/shard_map/dot_general | solution.py:20
  21.1 0.3 fusion.41
  21.4 0.0 copy-start.1
  21.4 1.0 fusion.8
  22.4 0.9 copy-done.1
  23.3 1.0 fusion.33
  24.3 0.0 collective-permute-done.1
  24.4 32.2 %collective-permute-done = bf16[256,2048]{1,0:T(8,128)(2,1)S(1)} collective-permute-done((bf16[256,2048]{1,0:T(8,128)(2,1)}, bf16[256,2048]{1,0:T(8,128)(2,1)S(1)}, u32[]{:S(2)}, u32[]{:S(2)}) %collective-permute-start) | collective-permute-done | bytes 1048608 | tf_op jit(solution)/shard_map/ppermute | solution.py:10
  56.5 1.0 fusion.22
  57.5 1.0 multiply_convert_fusion.7
  58.5 1.0 multiply_convert_fusion.1
  59.5 0.0 collective-permute-done.3
  59.5 0.5 fusion.40
  60.1 1.9 %collective-permute-start.4 = (bf16[256]{0:T(256)(128)(2,1)S(1)}, bf16[256]{0:T(256)(128)(2,1)S(1)}, u32[]{:S(2)}, u32[]{:S(2)}) collective-permute-start(bf16[256]{0:T(256)(128)(2,1)S(1)} %get-tuple-element.43), channel_id=1, source_target_pairs={{0,1},{1,2},{2,3},{3,4},{4,5},{5,6},{6,7},{7,8},{8,9},{9,10},{10,1... | collective-permute-start | bytes 1544 | tf_op jit(solution)/shard_map/ppermute | solution.py:10
  62.0 1.9 %collective-permute-start.2 = (bf16[256,2048]{1,0:T(8,128)(2,1)S(1)}, bf16[256,2048]{1,0:T(8,128)(2,1)S(1)}, u32[]{:S(2)}, u32[]{:S(2)}) collective-permute-start(bf16[256,2048]{1,0:T(8,128)(2,1)S(1)} %get-tuple-element.23), channel_id=1, source_target_pairs={{0,1},{1,2},{2,3},{3,4},{4,5},{5,6},{6,7},{7,8},{8,9},{9,10},{10,1... | collective-permute-start | bytes 3145736 | tf_op jit(solution)/shard_map/ppermute | solution.py:10
  63.9 1.3 %multiply_convert_fusion.4 = (bf16[256,768]{1,0:T(8,128)(2,1)S(1)}, bf16[256,768]{1,0:T(8,128)(2,1)S(1)}) fusion(f32[256,768]{1,0:T(8,128)S(1)} %fusion.22, f32[256,768]{1,0:T(8,128)S(1)} %get-tuple-element.28, bf16[256,2048]{1,0:T(8,128)(2,1)S(1)} %get-tuple-element.42, bf16[1,768,2048]{2,1,0:T(8,128)(2,1)S(1)} %copy-done), kind=kOutput, calls=%fused_computation.62 | convolution fusion | flops 807862272 | bytes 6553600 | tf_op jit(solution)/shard_map/dot_general | solution.py:20
  65.3 1.0 fusion.10
  66.3 1.0 fusion.36
  67.3 2.1 %collective-permute-start.5 = (bf16[256,2048]{1,0:T(8,128)(2,1)S(1)}, bf16[256,2048]{1,0:T(8,128)(2,1)S(1)}, u32[]{:S(2)}, u32[]{:S(2)}) collective-permute-start(bf16[256,2048]{1,0:T(8,128)(2,1)S(1)} %fusion.36), channel_id=1, source_target_pairs={{0,1},{1,2},{2,3},{3,4},{4,5},{5,6},{6,7},{7,8},{8,9},{9,10},{10,1... | collective-permute-start | bytes 3145736 | tf_op jit(solution)/shard_map/ppermute | solution.py:10
  69.4 0.1 constant_dynamic-update-slice_fusion
  69.5 3.5 %fusion.24 = bf16[1,2048,768]{2,1,0:T(8,128)(2,1)} fusion(bf16[512,2048]{1,0:T(8,128)(2,1)S(1)} %constant_dynamic-update-slice_fusion, bf16[256,768]{1,0:T(8,128)(2,1)S(1)} %get-tuple-element.35, bf16[256,768]{1,0:T(8,128)(2,1)S(1)} %get-tuple-element.34), kind=kOutput, calls=%fused_computation.27 | convolution fusion | flops 1613758464 | bytes 6029312 | tf_op jit(solution)/shard_map/dot_general | solution.py:14
  73.1 3.5 %fusion.25 = bf16[1,2048,768]{2,1,0:T(8,128)(2,1)} fusion(bf16[512,2048]{1,0:T(8,128)(2,1)S(1)} %constant_dynamic-update-slice_fusion, bf16[256,768]{1,0:T(8,128)(2,1)S(1)} %get-tuple-element.37, bf16[256,768]{1,0:T(8,128)(2,1)S(1)} %get-tuple-element.36), kind=kOutput, calls=%fused_computation.28 | convolution fusion | flops 1613758464 | bytes 6029312 | tf_op jit(solution)/shard_map/dot_general | solution.py:14
  76.6 3.5 %fusion.26 = bf16[1,768,2048]{2,1,0:T(8,128)(2,1)} fusion(bf16[256,2048]{1,0:T(8,128)(2,1)S(1)} %get-tuple-element.42, bf16[256,2048]{1,0:T(8,128)(2,1)S(1)} %fusion.46, bf16[256,768]{1,0:T(8,128)(2,1)S(1)} %get-tuple-element.22, bf16[256,768]{1,0:T(8,128)(2,1)S(1)} %get-tuple-element.24), kind=kOutput, calls=%fused_computation.29 | convolution fusion | flops 1617952768 | bytes 6029312 | tf_op jit(solution)/shard_map/dot_general | solution.py:14
  80.1 0.0 collective-permute-done.4
  80.1 0.5 convert_select_fusion
  80.6 20.9 %collective-permute-done.2 = bf16[256,2048]{1,0:T(8,128)(2,1)S(1)} collective-permute-done((bf16[256,2048]{1,0:T(8,128)(2,1)S(1)}, bf16[256,2048]{1,0:T(8,128)(2,1)S(1)}, u32[]{:S(2)}, u32[]{:S(2)}) %collective-permute-start.2) | collective-permute-done | bytes 1048608 | tf_op jit(solution)/shard_map/ppermute | solution.py:10
  101.5 11.2 %collective-permute-done.5 = bf16[256,2048]{1,0:T(8,128)(2,1)S(1)} collective-permute-done((bf16[256,2048]{1,0:T(8,128)(2,1)S(1)}, bf16[256,2048]{1,0:T(8,128)(2,1)S(1)}, u32[]{:S(2)}, u32[]{:S(2)}) %collective-permute-start.5) | collective-permute-done | bytes 1048608 | tf_op jit(solution)/shard_map/ppermute | solution.py:10
  112.7 1.6 %broadcast_select_fusion = (bf16[256,2048]{1,0:T(8,128)(2,1)}, bf16[256,2048]{1,0:T(8,128)(2,1)}) fusion(bf16[256,2048]{1,0:T(8,128)(2,1)S(1)} %collective-permute-done.5, bf16[256,2048]{1,0:T(8,128)(2,1)S(1)} %fusion.33, pred[256]{0:T(512)(128)(4,1)S(1)} %iota_compare_fusion, bf16[256,2048]{1,0:T(8,128)(2,1)S(1)} %collective-permute-done.2, ...), kind=kLoop, calls=%fused_computation.48 | loop fusion | flops 1048576 | bytes 6291712 | tf_op jit(solution)/shard_map/jit(_where)/select_n | solution.py:103
  (3 shorter events, 0.0 us)
Async XLA Ops:
  0.6 18.1 %copy-start = (bf16[1,768,2048]{2,1,0:T(8,128)(2,1)S(1)}, bf16[1,768,2048]{2,1,0:T(8,128)(2,1)}, u32[]{:S(2)}) copy-start(bf16[1,768,2048]{2,1,0:T(8,128)(2,1)} %param.13) | copy-start | bytes 9437188
  1.5 12.7 %copy-start.4 = (bf16[256,2048]{1,0:T(8,128)(2,1)S(1)}, bf16[256,2048]{1,0:T(8,128)(2,1)}, u32[]{:S(2)}) copy-start(bf16[256,2048]{1,0:T(8,128)(2,1)} %param.7) | copy-start | bytes 3145732
  2.3 22.0 %collective-permute-start.1 = (bf16[256]{0:T(256)(128)(2,1)S(1)}, bf16[256]{0:T(256)(128)(2,1)S(1)}, u32[]{:S(2)}, u32[]{:S(2)}) collective-permute-start(bf16[256]{0:T(256)(128)(2,1)S(1)} %get-tuple-element.47), channel_id=1, source_target_pairs={{1,0},{2,1},{3,2},{4,3},{5,4},{6,5},{7,6},{8,7},{9,8},{10,9},{11,1... | collective-permute-start | bytes 1544 | tf_op jit(solution)/shard_map/ppermute | solution.py:10
  6.9 52.6 %collective-permute-start.3 = (bf16[256,2048]{1,0:T(8,128)(2,1)}, bf16[256,2048]{1,0:T(8,128)(2,1)S(1)}, u32[]{:S(2)}, u32[]{:S(2)}) collective-permute-start(bf16[256,2048]{1,0:T(8,128)(2,1)} %param.9), channel_id=1, source_target_pairs={{1,0},{2,1},{3,2},{4,3},{5,4},{6,5},{7,6},{8,7},{9,8},{10,9},{11,1... | collective-permute-start | bytes 3145736 | tf_op jit(solution)/shard_map/ppermute | solution.py:10
  9.4 47.1 %collective-permute-start = (bf16[256,2048]{1,0:T(8,128)(2,1)}, bf16[256,2048]{1,0:T(8,128)(2,1)S(1)}, u32[]{:S(2)}, u32[]{:S(2)}) collective-permute-start(bf16[256,2048]{1,0:T(8,128)(2,1)} %param.7), channel_id=1, source_target_pairs={{1,0},{2,1},{3,2},{4,3},{5,4},{6,5},{7,6},{8,7},{9,8},{10,9},{11,1... | collective-permute-start | bytes 3145736 | tf_op jit(solution)/shard_map/ppermute | solution.py:10
  14.1 3.1 %copy-start.2 = (bf16[1,2048,768]{2,1,0:T(8,128)(2,1)S(1)}, bf16[1,2048,768]{2,1,0:T(8,128)(2,1)}, u32[]{:S(2)}) copy-start(bf16[1,2048,768]{2,1,0:T(8,128)(2,1)} %param.12) | copy-start | bytes 9437188
  17.2 1.2 %copy-start.3 = (bf16[256,2048]{1,0:T(8,128)(2,1)S(1)}, bf16[256,2048]{1,0:T(8,128)(2,1)}, u32[]{:S(2)}) copy-start(bf16[256,2048]{1,0:T(8,128)(2,1)} %param.9) | copy-start | bytes 3145732
  21.4 1.9 %copy-start.1 = (bf16[1,2048,768]{2,1,0:T(8,128)(2,1)S(1)}, bf16[1,2048,768]{2,1,0:T(8,128)(2,1)}, u32[]{:S(2)}) copy-start(bf16[1,2048,768]{2,1,0:T(8,128)(2,1)} %param.11) | copy-start | bytes 9437188
  60.1 20.0 %collective-permute-start.4 = (bf16[256]{0:T(256)(128)(2,1)S(1)}, bf16[256]{0:T(256)(128)(2,1)S(1)}, u32[]{:S(2)}, u32[]{:S(2)}) collective-permute-start(bf16[256]{0:T(256)(128)(2,1)S(1)} %get-tuple-element.43), channel_id=1, source_target_pairs={{0,1},{1,2},{2,3},{3,4},{4,5},{5,6},{6,7},{7,8},{8,9},{9,10},{10,1... | collective-permute-start | bytes 1544 | tf_op jit(solution)/shard_map/ppermute | solution.py:10
  62.0 39.5 %collective-permute-start.2 = (bf16[256,2048]{1,0:T(8,128)(2,1)S(1)}, bf16[256,2048]{1,0:T(8,128)(2,1)S(1)}, u32[]{:S(2)}, u32[]{:S(2)}) collective-permute-start(bf16[256,2048]{1,0:T(8,128)(2,1)S(1)} %get-tuple-element.23), channel_id=1, source_target_pairs={{0,1},{1,2},{2,3},{3,4},{4,5},{5,6},{6,7},{7,8},{8,9},{9,10},{10,1... | collective-permute-start | bytes 3145736 | tf_op jit(solution)/shard_map/ppermute | solution.py:10
  67.3 45.4 %collective-permute-start.5 = (bf16[256,2048]{1,0:T(8,128)(2,1)S(1)}, bf16[256,2048]{1,0:T(8,128)(2,1)S(1)}, u32[]{:S(2)}, u32[]{:S(2)}) collective-permute-start(bf16[256,2048]{1,0:T(8,128)(2,1)S(1)} %fusion.36), channel_id=1, source_target_pairs={{0,1},{1,2},{2,3},{3,4},{4,5},{5,6},{6,7},{7,8},{8,9},{9,10},{10,1... | collective-permute-start | bytes 3145736 | tf_op jit(solution)/shard_map/ppermute | solution.py:10

commit v2 on v1

v2 whole, which is shorter than its diff:
```python
import jax
import jax.numpy as jnp
from jax import lax
from jax.experimental import pallas as pl
from jax.experimental.pallas import tpu as pltpu
from jax.sharding import PartitionSpec as P


AXES = ("rows", "grp")
TAIL_SHARE = 4


def from_behind(block, distance):
    devices = range(lax.axis_size(AXES))
    route = [(i - distance, i) for i in devices if i - distance in devices]
    return lax.ppermute(block, AXES, route)


def contract_rows(left, right):
    return lax.dot_general(
        left, right, (((0,), (0,)), ((), ())), preferred_element_type=jnp.float32
    )


def contract_cols(left, right):
    return lax.dot_general(
        left, right, (((1,), (1,)), ((), ())), preferred_element_type=jnp.float32
    )


def expert_up(rows_in, gate_w, up_w):
    gate_pre = jnp.dot(rows_in, gate_w, preferred_element_type=jnp.float32)
    up_pre = jnp.dot(rows_in, up_w, preferred_element_type=jnp.float32)
    hidden = (gate_pre * jax.nn.sigmoid(gate_pre) * up_pre).astype(jnp.bfloat16)
    return lax.optimization_barrier((gate_pre, up_pre, hidden))


def expert_down(hidden, scale_col, down_w):
    expert_out = jnp.dot(hidden, down_w, preferred_element_type=jnp.float32)
    mixed = (scale_col * expert_out).astype(jnp.bfloat16)
    return lax.optimization_barrier((expert_out, mixed))


def output_grad(expert_out, scale_col, cotan_rows, keep):
    cotan_wide = cotan_rows.astype(jnp.float32)
    comb_grad = jnp.sum(expert_out * cotan_wide, axis=1).astype(jnp.bfloat16)
    out_grad = (scale_col * cotan_wide).astype(jnp.bfloat16)
    if keep is not None:
        out_grad = jnp.where(keep[:, None], out_grad, jnp.zeros_like(out_grad))
    return comb_grad, out_grad


def expert_back(out_grad, gate_pre, up_pre, gate_w, up_w, down_w):
    sig_gate = jax.nn.sigmoid(gate_pre)
    silu_gate = gate_pre * sig_gate
    hidden_grad = contract_cols(out_grad, down_w)
    gate_grad = (hidden_grad * up_pre * sig_gate * (1.0 + gate_pre * (1.0 - sig_gate))).astype(
        jnp.bfloat16
    )
    up_grad = (hidden_grad * silu_gate).astype(jnp.bfloat16)
    in_grad = (contract_cols(gate_grad, gate_w) + contract_cols(up_grad, up_w)).astype(jnp.bfloat16)
    return lax.optimization_barrier((gate_grad, up_grad, in_grad))


def join_tail(lead_count, back, own_tail, whole, start):
    rows, cols = back.shape

    def kernel(lead_ref, back_ref, own_ref, whole_ref, out_ref):
        row = start + lax.broadcasted_iota(jnp.int32, (rows, cols), 0)
        out_ref[...] = jnp.where(row < lead_ref[0], back_ref[...], own_ref[...])

    resident = pl.BlockSpec(memory_space=pltpu.VMEM)
    return pl.pallas_call(
        kernel,
        out_shape=jax.ShapeDtypeStruct(whole.shape, whole.dtype),
        grid_spec=pltpu.PrefetchScalarGridSpec(
            num_scalar_prefetch=1,
            grid=(1,),
            in_specs=[resident, resident, pl.BlockSpec(memory_space=pl.ANY)],
            out_specs=pl.BlockSpec((rows, cols), lambda i, lead: (start // rows, 0)),
        ),
        input_output_aliases={3: 0},
        name="join_tail",
    )(lead_count[None], back, own_tail, whole)


def device_step(sorted_rows, combine, cotangent, starts, w_gate, w_up, w_down):
    gate_w, up_w, down_w = w_gate[0], w_up[0], w_down[0]
    count_rows = sorted_rows.shape[0]
    cut = count_rows - count_rows // TAIL_SHARE
    pieces = [slice(0, cut), slice(cut, count_rows)]
    lead_count = jnp.remainder(starts[0], count_rows)
    lead_mask = jnp.arange(count_rows, dtype=jnp.int32) < lead_count
    own_mask = jnp.logical_not(lead_mask)

    next_rows = from_behind(sorted_rows, -1)
    next_comb = from_behind(jnp.where(lead_mask, combine, jnp.zeros_like(combine)), -1)
    next_cotan = []
    for piece in pieces:
        next_cotan.append(from_behind(cotangent[piece], -1))

    own_scale = combine.astype(jnp.float32)[:, None]
    own_gate, own_up, own_hidden = expert_up(sorted_rows, gate_w, up_w)
    own_out, own_mixed = expert_down(own_hidden, own_scale, down_w)
    own_comb_grad, own_out_grad = output_grad(own_out, own_scale, cotangent, own_mask)
    own_gate_grad, own_up_grad, own_in_grad = expert_back(
        own_out_grad, own_gate, own_up, gate_w, up_w, down_w
    )

    next_scale = next_comb.astype(jnp.float32)[:, None]
    next_gate, next_up, next_hidden = expert_up(next_rows, gate_w, up_w)
    next_out, next_mixed = expert_down(next_hidden, next_scale, down_w)
    back_mixed = from_behind(next_mixed, 1)

    next_comb_grad, next_out_grad, next_gate_grad, next_up_grad, back_in = [], [], [], [], []
    for p, piece in enumerate(pieces):
        comb_grad, out_grad = output_grad(next_out[piece], next_scale[piece], next_cotan[p], None)
        gate_grad, up_grad, in_grad = expert_back(
            out_grad, next_gate[piece], next_up[piece], gate_w, up_w, down_w
        )
        next_out, next_gate, next_up, in_grad = lax.optimization_barrier(
            (next_out, next_gate, next_up, in_grad)
        )
        next_comb_grad.append(comb_grad)
        next_out_grad.append(out_grad)
        next_gate_grad.append(gate_grad)
        next_up_grad.append(up_grad)
        back_in.append(from_behind(in_grad, 1))
    back_comb_grad = from_behind(jnp.concatenate(next_comb_grad), 1)

    rows_all = jnp.concatenate([sorted_rows, next_rows], axis=0)
    hidden_all = jnp.concatenate([own_hidden, next_hidden], axis=0)
    out_grad_all = jnp.concatenate([own_out_grad] + next_out_grad, axis=0)
    gate_grad_all = jnp.concatenate([own_gate_grad] + next_gate_grad, axis=0)
    up_grad_all = jnp.concatenate([own_up_grad] + next_up_grad, axis=0)
    grad_gate = contract_rows(rows_all, gate_grad_all)[None].astype(jnp.bfloat16)
    grad_up = contract_rows(rows_all, up_grad_all)[None].astype(jnp.bfloat16)
    grad_down = contract_rows(hidden_all, out_grad_all)[None].astype(jnp.bfloat16)

    mixed = lax.optimization_barrier(jnp.where(lead_mask[:, None], back_mixed, own_mixed))
    head, tail = pieces
    joined = jnp.where(lead_mask[head][:, None], back_in[0], own_in_grad[head])
    in_grad = lax.optimization_barrier(jnp.concatenate([joined, own_in_grad[tail]]))
    in_grad = join_tail(lead_count, back_in[1], own_in_grad[tail], in_grad, tail.start)
    comb_grad = jnp.where(lead_mask, back_comb_grad, own_comb_grad)
    return (mixed, comb_grad, in_grad, grad_gate, grad_up, grad_down)


def solution(mesh):
    rows_1d, rows_2d, rows_3d = P(AXES), P(AXES, None), P(AXES, None, None)
    return jax.shard_map(
        device_step,
        mesh=mesh,
        in_specs=(rows_2d, rows_1d, rows_2d, rows_1d, rows_3d, rows_3d, rows_3d),
        out_specs=(rows_2d, rows_1d, rows_2d, rows_3d, rows_3d, rows_3d),
        check_vma=False,
    )
```

time: 115 us -> 108 us (0.939); the launches traced: 114 us -> 106 us
  waiting for transfers between devices: 64.3 us -> 41.6 us
  starting transfers between devices: 16.4 us -> 22.1 us
  matrix products: 25.4 us -> 28.8 us
  other arithmetic: 4.07 us -> 6.45 us
  Pallas kernels: 0 us -> 1.76 us
    ppermute x6 -> x8, waiting for transfers between devices: 64.3 us -> 41.6 us  [from_behind(): return lax.ppermute(block, AXES, route)]
    ppermute x6 -> x8, starting transfers between devices: 16.4 us -> 22.1 us  [from_behind(): return lax.ppermute(block, AXES, route)]
    dot_general x6 -> x9, matrix products: 6.73 us -> 10.3 us  [contract_cols(): lax.dot_general(left, right, (((1,), (1,)), ((), ())), preferred_element_...]
    slice x0 -> x5, local copies, waits for them, and re-layouts: none -> 2.27 us  [the longest x2 2.17 us: device_step(): next_cotan.append(from_behind(cotangent[piece], -1))]
    dot_general x2, matrix products: 4.01 us -> 1.96 us  [expert_up(): gate_pre = jnp.dot(rows_in, gate_w, preferred_element_type=jnp.float32)]
    dot_general x2, matrix products: 2.04 us -> 3.99 us  [expert_down(): expert_out = jnp.dot(hidden, down_w, preferred_element_type=jnp.float32)]
    pallas_call x0 -> x1, Pallas kernels: none -> 1.76 us  [join_tail(): pl.pallas_call(kernel, out_shape=jax.ShapeDtypeStruct(whole.shape, whole....]
    unnamed x11 -> x13, local copies, waits for them, and re-layouts: 2.45 us -> 1.03 us
  transfers between devices with their start and end apart: 6 -> 8, of which waited for: 3 -> 4; matrix products, arithmetic and copies ran while one was open for 24% -> 32% of each run, Pallas kernels for 0% -> 2%
where the time goes in v2:
time: 108 us; the launch traced here: 106 us
  waiting for transfers between devices  41.6 us (39%)
  matrix products  28.8 us (27%)
  starting transfers between devices  22.1 us (20%)
  other arithmetic  6.45 us (6%)
  local copies, waits for them, and re-layouts  3.39 us (3%)
  between operations  1.77 us (2%)
  Pallas kernels  1.76 us (2%)
    ppermute x8, waiting for transfers between devices, from_behind(): return lax.ppermute(block, AXES, route)  41.6 us
    ppermute x8, starting transfers between devices, from_behind(): return lax.ppermute(block, AXES, route)  22.1 us
    dot_general x3, matrix products, contract_rows(): lax.dot_general(left, right, (((0,), (0,)), ((), ())), preferred_element_...  10.6 us
    dot_general x9, matrix products, contract_cols(): lax.dot_general(left, right, (((1,), (1,)), ((), ())), preferred_element_...  10.3 us
    dot_general x2, matrix products, expert_down(): expert_out = jnp.dot(hidden, down_w, preferred_element_type=jnp.float32)  3.99 us
    select_n x1, other arithmetic, device_step(): jnp.where(lead_mask[:, None], back_mixed, own_mixed)  2.68 us
    slice x2, local copies, waits for them, and re-layouts, device_step(): next_cotan.append(from_behind(cotangent[piece], -1))  2.17 us
  transfers between devices with their start and end apart: 8, of which 4 were waited for; matrix products, arithmetic and copies ran while one was open for 32% of the time, Pallas kernels for 2%

profile of v2, /device:TPU:17, one launch (start us, length us, event | category | flops | bytes accessed | tf_op | source)
XLA Modules:
  0.0 105.9 jit_solution(14659610881144773386)
XLA Ops:
  0.6 0.0 copy-start
  1.5 0.8 fusion.80
  2.3 4.9 %collective-permute-start.1 = (bf16[256]{0:T(256)(128)(2,1)S(1)}, bf16[256]{0:T(256)(128)(2,1)S(1)}, u32[]{:S(2)}, u32[]{:S(2)}) collective-permute-start(bf16[256]{0:T(256)(128)(2,1)S(1)} %get-tuple-element.65), channel_id=1, source_target_pairs={{1,0},{2,1},{3,2},{4,3},{5,4},{6,5},{7,6},{8,7},{9,8},{10,9},{11,1... | collective-permute-start | bytes 1544 | tf_op jit(solution)/shard_map/ppermute | solution.py:16
  7.2 2.4 %collective-permute-start = (bf16[256,2048]{1,0:T(8,128)(2,1)}, bf16[256,2048]{1,0:T(8,128)(2,1)S(1)}, u32[]{:S(2)}, u32[]{:S(2)}) collective-permute-start(bf16[256,2048]{1,0:T(8,128)(2,1)} %param.7), channel_id=1, source_target_pairs={{1,0},{2,1},{3,2},{4,3},{5,4},{6,5},{7,6},{8,7},{9,8},{10,9},{11,1... | collective-permute-start | bytes 3145736 | tf_op jit(solution)/shard_map/ppermute | solution.py:16
  9.6 1.0 slice.48
  10.6 3.3 %collective-permute-start.4 = (bf16[64,2048]{1,0:T(8,128)(2,1)S(1)}, bf16[64,2048]{1,0:T(8,128)(2,1)S(1)}, u32[]{:S(2)}, u32[]{:S(2)}) collective-permute-start(bf16[64,2048]{1,0:T(8,128)(2,1)S(1)} %slice.48), channel_id=1, source_target_pairs={{1,0},{2,1},{3,2},{4,3},{5,4},{6,5},{7,6},{8,7},{9,8},{10,9},{11,1... | collective-permute-start | bytes 786440 | tf_op jit(solution)/shard_map/ppermute | solution.py:16
  14.0 1.2 %slice.43 = bf16[192,2048]{1,0:T(8,128)(2,1)S(1)} slice(bf16[256,2048]{1,0:T(8,128)(2,1)} %param.9), slice={[0:192], [0:2048]} | slice | bytes 1572864 | tf_op jit(solution)/shard_map/slice | solution.py:100
  15.2 2.4 %collective-permute-start.3 = (bf16[192,2048]{1,0:T(8,128)(2,1)S(1)}, bf16[192,2048]{1,0:T(8,128)(2,1)S(1)}, u32[]{:S(2)}, u32[]{:S(2)}) collective-permute-start(bf16[192,2048]{1,0:T(8,128)(2,1)S(1)} %slice.43), channel_id=1, source_target_pairs={{1,0},{2,1},{3,2},{4,3},{5,4},{6,5},{7,6},{8,7},{9,8},{10,9},{11,1... | collective-permute-start | bytes 2359304 | tf_op jit(solution)/shard_map/ppermute | solution.py:16
  17.7 0.1 constant_dynamic-update-slice_fusion.1
  17.8 1.0 fusion.26
  18.8 0.9 copy-done.1
  19.7 1.0 multiply_convert_fusion.4
  20.7 2.0 %multiply_convert_fusion = (bf16[256,2048]{1,0:T(8,128)(2,1)}, f32[256,2048]{1,0:T(8,128)S(1)}) fusion(f32[256]{0:T(256)S(1)} %get-tuple-element.64, bf16[256,768]{1,0:T(8,128)(2,1)S(1)} %get-tuple-element.32, bf16[1,768,2048]{2,1,0:T(8,128)(2,1)S(1)} %copy-done), kind=kOutput, calls=%fused_computation.51 | convolution fusion | flops 806354944 | bytes 6685696 | tf_op jit(solution)/shard_map/dot_general | solution.py:39
  22.7 0.3 fusion.60
  23.0 1.3 %multiply_convert_fusion.2 = (bf16[256,768]{1,0:T(8,128)(2,1)S(1)}, bf16[256,768]{1,0:T(8,128)(2,1)S(1)}) fusion(f32[256,768]{1,0:T(8,128)S(1)} %fusion.26, f32[256,768]{1,0:T(8,128)S(1)} %get-tuple-element.44, bf16[256,2048]{1,0:T(8,128)(2,1)S(1)} %fusion.60, bf16[1,768,2048]{2,1,0:T(8,128)(2,1)S(1)} %copy-done), kind=kOutput, calls=%fused_computation.74 | convolution fusion | flops 807862272 | bytes 6553600 | tf_op jit(solution)/shard_map/dot_general | solution.py:26
  24.4 0.3 fusion.51
  24.7 1.0 fusion.10
  25.7 1.0 fusion.36
  26.8 0.1 slice.49
  26.8 18.4 %collective-permute-done = bf16[256,2048]{1,0:T(8,128)(2,1)S(1)} collective-permute-done((bf16[256,2048]{1,0:T(8,128)(2,1)}, bf16[256,2048]{1,0:T(8,128)(2,1)S(1)}, u32[]{:S(2)}, u32[]{:S(2)}) %collective-permute-start) | collective-permute-done | bytes 1048608 | tf_op jit(solution)/shard_map/ppermute | solution.py:16
  45.2 1.0 fusion.28
  46.2 1.0 multiply_convert_fusion.5
  47.2 2.0 %multiply_convert_fusion.1 = (bf16[256,2048]{1,0:T(8,128)(2,1)}, f32[256,2048]{1,0:T(8,128)S(1)}) fusion(f32[256]{0:T(256)S(1)} %convert_element_type.91, bf16[256,768]{1,0:T(8,128)(2,1)S(1)} %get-tuple-element.30, bf16[1,768,2048]{2,1,0:T(8,128)(2,1)S(1)} %copy-done), kind=kOutput, calls=%fused_computation.52 | convolution fusion | flops 806354944 | bytes 6685696 | tf_op jit(solution)/shard_map/dot_general | solution.py:39
  49.2 1.9 %collective-permute-start.2 = (bf16[256,2048]{1,0:T(8,128)(2,1)}, bf16[256,2048]{1,0:T(8,128)(2,1)}, u32[]{:S(2)}, u32[]{:S(2)}) collective-permute-start(bf16[256,2048]{1,0:T(8,128)(2,1)} %get-tuple-element.31), channel_id=1, source_target_pairs={{0,1},{1,2},{2,3},{3,4},{4,5},{5,6},{6,7},{7,8},{8,9},{9,10},{10,1... | collective-permute-start | bytes 3145736 | tf_op jit(solution)/shard_map/ppermute | solution.py:16
  51.1 15.4 %collective-permute-done.3 = bf16[192,2048]{1,0:T(8,128)(2,1)S(1)} collective-permute-done((bf16[192,2048]{1,0:T(8,128)(2,1)S(1)}, bf16[192,2048]{1,0:T(8,128)(2,1)S(1)}, u32[]{:S(2)}, u32[]{:S(2)}) %collective-permute-start.3) | collective-permute-done | bytes 786464 | tf_op jit(solution)/shard_map/ppermute | solution.py:16
  66.5 0.4 fusion.58
  66.9 1.4 %multiply_convert_fusion.6 = (bf16[192,768]{1,0:T(8,128)(2,1)S(1)}, bf16[192,768]{1,0:T(8,128)(2,1)S(1)}) fusion(f32[256,768]{1,0:T(8,128)S(1)} %fusion.28, f32[256,768]{1,0:T(8,128)S(1)} %get-tuple-element.41, bf16[192,2048]{1,0:T(8,128)(2,1)S(1)} %get-tuple-element.61, bf16[1,768,2048]{2,1,0:T(8,128)(2,1)S(1)} %copy-done), kind=kOutput, calls=%fused_computation.81 | convolution fusion | flops 605896704 | bytes 5701632 | tf_op jit(solution)/shard_map/dot_general | solution.py:26
  68.3 1.2 %fusion.14 = f32[192,2048]{1,0:T(8,128)S(1)} fusion(bf16[192,768]{1,0:T(8,128)(2,1)S(1)} %get-tuple-element.52, bf16[1,2048,768]{2,1,0:T(8,128)(2,1)S(1)} %copy-done.1), kind=kOutput, calls=%fused_computation.17 | convolution fusion | flops 603979776 | bytes 5013504 | tf_op jit(solution)/shard_map/dot_general | solution.py:26
  69.4 1.2 %fusion.42 = bf16[192,2048]{1,0:T(8,128)(2,1)S(1)} fusion(f32[192,2048]{1,0:T(8,128)S(1)} %fusion.14, bf16[192,768]{1,0:T(8,128)(2,1)S(1)} %get-tuple-element.49, bf16[1,2048,768]{2,1,0:T(8,128)(2,1)S(1)} %copy-done.2), kind=kOutput, calls=%fused_computation.41 | convolution fusion | flops 604766208 | bytes 5799936 | tf_op jit(solution)/shard_map/dot_general | solution.py:26
  70.6 0.2 fusion.75
  70.8 0.1 pad_maximum_fusion.1
  70.9 2.1 %collective-permute-start.5 = (bf16[256]{0:T(256)(128)(2,1)S(1)}, bf16[256]{0:T(256)(128)(2,1)S(1)}, u32[]{:S(2)}, u32[]{:S(2)}) collective-permute-start(bf16[256]{0:T(256)(128)(2,1)S(1)} %pad_maximum_fusion.1), channel_id=1, source_target_pairs={{0,1},{1,2},{2,3},{3,4},{4,5},{5,6},{6,7},{7,8},{8,9},{9,10},{10,1... | collective-permute-start | bytes 1544 | tf_op jit(solution)/shard_map/ppermute | solution.py:16
  73.0 1.1 %multiply_convert_fusion.8 = (bf16[64,768]{1,0:T(8,128)(2,1)S(1)}, bf16[64,768]{1,0:T(8,128)(2,1)S(1)}) fusion(f32[256,768]{1,0:T(8,128)S(1)} %fusion.28, f32[256,768]{1,0:T(8,128)S(1)} %get-tuple-element.41, bf16[64,2048]{1,0:T(8,128)(2,1)S(1)} %get-tuple-element.62, bf16[1,768,2048]{2,1,0:T(8,128)(2,1)S(1)} %copy-done), kind=kOutput, calls=%fused_computation.86 | convolution fusion | flops 201965568 | bytes 3997696 | tf_op jit(solution)/shard_map/dot_general | solution.py:26
  74.1 1.1 fusion.12
  75.1 1.1 %fusion.48 = bf16[64,2048]{1,0:T(8,128)(2,1)S(1)} fusion(f32[64,2048]{1,0:T(8,128)S(1)} %fusion.12, bf16[64,768]{1,0:T(8,128)(2,1)S(1)} %get-tuple-element.50, bf16[1,2048,768]{2,1,0:T(8,128)(2,1)S(1)} %copy-done.2), kind=kOutput, calls=%fused_computation.43 | convolution fusion | flops 201588736 | bytes 4030464 | tf_op jit(solution)/shard_map/dot_general | solution.py:26
  76.2 3.1 %collective-permute-start.7 = (bf16[192,2048]{1,0:T(8,128)(2,1)S(1)}, bf16[192,2048]{1,0:T(8,128)(2,1)S(1)}, u32[]{:S(2)}, u32[]{:S(2)}) collective-permute-start(bf16[192,2048]{1,0:T(8,128)(2,1)S(1)} %fusion.42), channel_id=1, source_target_pairs={{0,1},{1,2},{2,3},{3,4},{4,5},{5,6},{6,7},{7,8},{8,9},{9,10},{10,1... | collective-permute-start | bytes 2359304 | tf_op jit(solution)/shard_map/ppermute | solution.py:16
  79.3 0.1 constant_dynamic-update-slice_fusion
  79.4 3.5 %fusion.30 = bf16[1,2048,768]{2,1,0:T(8,128)(2,1)} fusion(bf16[512,2048]{1,0:T(8,128)(2,1)S(1)} %constant_dynamic-update-slice_fusion, bf16[64,768]{1,0:T(8,128)(2,1)S(1)} %get-tuple-element.50, bf16[192,768]{1,0:T(8,128)(2,1)S(1)} %get-tuple-element.49, bf16[256,768]{1,0:T(8,128)(2,1)S(1)} %get-tuple-element.48), kind=kOutput, calls=%fused_computation.33 | convolution fusion | flops 1614544896 | bytes 6029312 | tf_op jit(solution)/shard_map/dot_general | solution.py:20
  82.9 3.5 %fusion.31 = bf16[1,2048,768]{2,1,0:T(8,128)(2,1)} fusion(bf16[512,2048]{1,0:T(8,128)(2,1)S(1)} %constant_dynamic-update-slice_fusion, bf16[64,768]{1,0:T(8,128)(2,1)S(1)} %get-tuple-element.53, bf16[192,768]{1,0:T(8,128)(2,1)S(1)} %get-tuple-element.52, bf16[256,768]{1,0:T(8,128)(2,1)S(1)} %get-tuple-element.51), kind=kOutput, calls=%fused_computation.34 | convolution fusion | flops 1614544896 | bytes 6029312 | tf_op jit(solution)/shard_map/dot_general | solution.py:20
  86.5 3.5 %fusion.32 = bf16[1,768,2048]{2,1,0:T(8,128)(2,1)} fusion(bf16[64,2048]{1,0:T(8,128)(2,1)S(1)} %get-tuple-element.62, bf16[192,2048]{1,0:T(8,128)(2,1)S(1)} %get-tuple-element.61, bf16[256,2048]{1,0:T(8,128)(2,1)S(1)} %fusion.60, bf16[256,768]{1,0:T(8,128)(2,1)S(1)} %get-tuple-element.30, bf16[256,768]{1,0:T(8,128)(2,1)S(1)} %get-tuple-element.32), kind=kOutput, calls=%fused_computation.35 | convolution fusion | flops 1620049920 | bytes 6029312 | tf_op jit(solution)/shard_map/dot_general | solution.py:20
  90.0 1.9 %collective-permute-start.6 = (bf16[64,2048]{1,0:T(8,128)(2,1)S(1)}, bf16[64,2048]{1,0:T(8,128)(2,1)}, u32[]{:S(2)}, u32[]{:S(2)}) collective-permute-start(bf16[64,2048]{1,0:T(8,128)(2,1)S(1)} %fusion.48), channel_id=1, source_target_pairs={{0,1},{1,2},{2,3},{3,4},{4,5},{5,6},{6,7},{7,8},{8,9},{9,10},{10,1... | collective-permute-start | bytes 786440 | tf_op jit(solution)/shard_map/ppermute | solution.py:16
  91.9 0.5 convert_select_fusion
  92.4 3.0 %collective-permute-done.7 = bf16[192,2048]{1,0:T(8,128)(2,1)S(1)} collective-permute-done((bf16[192,2048]{1,0:T(8,128)(2,1)S(1)}, bf16[192,2048]{1,0:T(8,128)(2,1)S(1)}, u32[]{:S(2)}, u32[]{:S(2)}) %collective-permute-start.7) | collective-permute-done | bytes 786464 | tf_op jit(solution)/shard_map/ppermute | solution.py:16
  95.4 0.1 slice_select_fusion
  95.5 1.1 %pad_maximum_fusion.whole_ref = bf16[256,2048]{1,0:T(8,128)(2,1)} fusion(bf16[64,2048]{1,0:T(8,128)(2,1)S(1)} %slice.52.own_ref, bf16[192,2048]{1,0:T(8,128)(2,1)S(1)} %slice_select_fusion), kind=kLoop, calls=%fused_computation.58 | loop fusion | flops 2097152 | bytes 2097152 | tf_op jit(solution)/shard_map/concatenate | solution.py:143
  96.6 4.9 %collective-permute-done.6.back_ref = bf16[64,2048]{1,0:T(8,128)(2,1)} collective-permute-done((bf16[64,2048]{1,0:T(8,128)(2,1)S(1)}, bf16[64,2048]{1,0:T(8,128)(2,1)}, u32[]{:S(2)}, u32[]{:S(2)}) %collective-permute-start.6) | collective-permute-done | bytes 262176 | tf_op jit(solution)/shard_map/ppermute | solution.py:16
  101.5 1.8 %join_tail.1 = bf16[256,2048]{1,0:T(8,128)(2,1)} custom-call(s32[1]{0:T(128)} %bitcast.4.lead_ref, bf16[64,2048]{1,0:T(8,128)(2,1)} %collective-permute-done.6.back_ref, bf16[64,2048]{1,0:T(8,128)(2,1)} %copy-done.4, bf16[256,2048]{1,0:T(8,128)(2,1)} %pad_maximum_fusion.whole_ref), custom_call_target="tpu_custom_call", output_to_operand_aliasing={{}: (3, {})} | custom-call | tf_op jit(solution)/shard_map/join_tail/pallas_call | solution.py:73
  103.3 2.7 %broadcast_select_fusion = bf16[256,2048]{1,0:T(8,128)(2,1)} fusion(bf16[256,2048]{1,0:T(8,128)(2,1)} %collective-permute-done.2, bf16[256,2048]{1,0:T(8,128)(2,1)} %get-tuple-element.33, pred[256]{0:T(512)(128)(4,1)S(1)} %iota_compare_fusion), kind=kLoop, calls=%fused_computation.59 | loop fusion | flops 524288 | bytes 3145984 | tf_op jit(solution)/shard_map/jit(_where)/select_n | solution.py:140
  (19 shorter events, 0.1 us)
Async XLA Ops:
  0.6 20.1 %copy-start = (bf16[1,768,2048]{2,1,0:T(8,128)(2,1)S(1)}, bf16[1,768,2048]{2,1,0:T(8,128)(2,1)}, u32[]{:S(2)}) copy-start(bf16[1,768,2048]{2,1,0:T(8,128)(2,1)} %param.13) | copy-start | bytes 9437188
  1.5 16.2 %copy-start.5 = (bf16[256,2048]{1,0:T(8,128)(2,1)S(1)}, bf16[256,2048]{1,0:T(8,128)(2,1)}, u32[]{:S(2)}) copy-start(bf16[256,2048]{1,0:T(8,128)(2,1)} %param.7) | copy-start | bytes 3145732
  2.3 15.5 %copy-start.2 = (bf16[1,2048,768]{2,1,0:T(8,128)(2,1)S(1)}, bf16[1,2048,768]{2,1,0:T(8,128)(2,1)}, u32[]{:S(2)}) copy-start(bf16[1,2048,768]{2,1,0:T(8,128)(2,1)} %param.11) | copy-start | bytes 9437188
  2.3 24.4 %collective-permute-start.1 = (bf16[256]{0:T(256)(128)(2,1)S(1)}, bf16[256]{0:T(256)(128)(2,1)S(1)}, u32[]{:S(2)}, u32[]{:S(2)}) collective-permute-start(bf16[256]{0:T(256)(128)(2,1)S(1)} %get-tuple-element.65), channel_id=1, source_target_pairs={{1,0},{2,1},{3,2},{4,3},{5,4},{6,5},{7,6},{8,7},{9,8},{10,9},{11,1... | collective-permute-start | bytes 1544 | tf_op jit(solution)/shard_map/ppermute | solution.py:16
  7.2 38.0 %collective-permute-start = (bf16[256,2048]{1,0:T(8,128)(2,1)}, bf16[256,2048]{1,0:T(8,128)(2,1)S(1)}, u32[]{:S(2)}, u32[]{:S(2)}) collective-permute-start(bf16[256,2048]{1,0:T(8,128)(2,1)} %param.7), channel_id=1, source_target_pairs={{1,0},{2,1},{3,2},{4,3},{5,4},{6,5},{7,6},{8,7},{9,8},{10,9},{11,1... | collective-permute-start | bytes 3145736 | tf_op jit(solution)/shard_map/ppermute | solution.py:16
  10.6 60.0 %collective-permute-start.4 = (bf16[64,2048]{1,0:T(8,128)(2,1)S(1)}, bf16[64,2048]{1,0:T(8,128)(2,1)S(1)}, u32[]{:S(2)}, u32[]{:S(2)}) collective-permute-start(bf16[64,2048]{1,0:T(8,128)(2,1)S(1)} %slice.48), channel_id=1, source_target_pairs={{1,0},{2,1},{3,2},{4,3},{5,4},{6,5},{7,6},{8,7},{9,8},{10,9},{11,1... | collective-permute-start | bytes 786440 | tf_op jit(solution)/shard_map/ppermute | solution.py:16
  15.2 51.3 %collective-permute-start.3 = (bf16[192,2048]{1,0:T(8,128)(2,1)S(1)}, bf16[192,2048]{1,0:T(8,128)(2,1)S(1)}, u32[]{:S(2)}, u32[]{:S(2)}) collective-permute-start(bf16[192,2048]{1,0:T(8,128)(2,1)S(1)} %slice.43), channel_id=1, source_target_pairs={{1,0},{2,1},{3,2},{4,3},{5,4},{6,5},{7,6},{8,7},{9,8},{10,9},{11,1... | collective-permute-start | bytes 2359304 | tf_op jit(solution)/shard_map/ppermute | solution.py:16
  17.8 1.9 %copy-start.1 = (bf16[1,2048,768]{2,1,0:T(8,128)(2,1)S(1)}, bf16[1,2048,768]{2,1,0:T(8,128)(2,1)}, u32[]{:S(2)}) copy-start(bf16[1,2048,768]{2,1,0:T(8,128)(2,1)} %param.12) | copy-start | bytes 9437188
  20.7 2.0 %copy-start.3 = (bf16[256,2048]{1,0:T(8,128)(2,1)S(1)}, bf16[256,2048]{1,0:T(8,128)(2,1)}, u32[]{:S(2)}) copy-start(bf16[256,2048]{1,0:T(8,128)(2,1)} %param.9) | copy-start | bytes 3145732
  26.7 68.8 %copy-start.4 = (bf16[64,2048]{1,0:T(8,128)(2,1)}, bf16[64,2048]{1,0:T(8,128)(2,1)S(1)}, u32[]{:S(2)}) copy-start(bf16[64,2048]{1,0:T(8,128)(2,1)S(1)} %slice.52.own_ref) | copy-start | bytes 786436
  49.2 54.0 %collective-permute-start.2 = (bf16[256,2048]{1,0:T(8,128)(2,1)}, bf16[256,2048]{1,0:T(8,128)(2,1)}, u32[]{:S(2)}, u32[]{:S(2)}) collective-permute-start(bf16[256,2048]{1,0:T(8,128)(2,1)} %get-tuple-element.31), channel_id=1, source_target_pairs={{0,1},{1,2},{2,3},{3,4},{4,5},{5,6},{6,7},{7,8},{8,9},{9,10},{10,1... | collective-permute-start | bytes 3145736 | tf_op jit(solution)/shard_map/ppermute | solution.py:16
  70.9 21.0 %collective-permute-start.5 = (bf16[256]{0:T(256)(128)(2,1)S(1)}, bf16[256]{0:T(256)(128)(2,1)S(1)}, u32[]{:S(2)}, u32[]{:S(2)}) collective-permute-start(bf16[256]{0:T(256)(128)(2,1)S(1)} %pad_maximum_fusion.1), channel_id=1, source_target_pairs={{0,1},{1,2},{2,3},{3,4},{4,5},{5,6},{6,7},{7,8},{8,9},{9,10},{10,1... | collective-permute-start | bytes 1544 | tf_op jit(solution)/shard_map/ppermute | solution.py:16
  76.2 19.2 %collective-permute-start.7 = (bf16[192,2048]{1,0:T(8,128)(2,1)S(1)}, bf16[192,2048]{1,0:T(8,128)(2,1)S(1)}, u32[]{:S(2)}, u32[]{:S(2)}) collective-permute-start(bf16[192,2048]{1,0:T(8,128)(2,1)S(1)} %fusion.42), channel_id=1, source_target_pairs={{0,1},{1,2},{2,3},{3,4},{4,5},{5,6},{6,7},{7,8},{8,9},{9,10},{10,1... | collective-permute-start | bytes 2359304 | tf_op jit(solution)/shard_map/ppermute | solution.py:16
  90.0 11.5 %collective-permute-start.6 = (bf16[64,2048]{1,0:T(8,128)(2,1)S(1)}, bf16[64,2048]{1,0:T(8,128)(2,1)}, u32[]{:S(2)}, u32[]{:S(2)}) collective-permute-start(bf16[64,2048]{1,0:T(8,128)(2,1)S(1)} %fusion.48), channel_id=1, source_target_pairs={{0,1},{1,2},{2,3},{3,4},{4,5},{5,6},{6,7},{7,8},{8,9},{9,10},{10,1... | collective-permute-start | bytes 786440 | tf_op jit(solution)/shard_map/ppermute | solution.py:16

commit v3 on v1

--- a/solution.py
+++ b/solution.py
@@ -98,9 +98,11 @@
     grad_up = contract_rows(rows_all, up_grad_all)[None].astype(jnp.bfloat16)
     grad_down = contract_rows(hidden_all, out_grad_all)[None].astype(jnp.bfloat16)
 
+    comb_grad = lax.optimization_barrier(jnp.where(lead_mask, back_comb_grad, own_comb_grad))
     mixed = jnp.where(lead_mask[:, None], back_mixed, own_mixed)
-    comb_grad = jnp.where(lead_mask, back_comb_grad, own_comb_grad)
-    in_grad = jnp.where(lead_mask[:, None], back_in_grad, own_in_grad)
+    mixed, own_in_grad = lax.optimization_barrier((mixed, own_in_grad))
+    row = lax.broadcasted_iota(jnp.int32, own_in_grad.shape, 0)
+    in_grad = jnp.where(row < lead_count, back_in_grad, own_in_grad)
     return (mixed, comb_grad, in_grad, grad_gate, grad_up, grad_down)
 
 

time: 115 us -> 114 us (level)
    select_n x2 -> x3, other arithmetic: 2.1 us -> 2.8 us  [the longest x1 1.14 us: device_step(): mixed = jnp.where(lead_mask[:, None], back_mixed, own_mixed)]
  transfers between devices with their start and end apart: 6 -> 6, of which waited for: 3 -> 3; matrix products, arithmetic and copies ran while one was open for 24% -> 25% of each run, Pallas kernels for 0% -> 0%
where the time goes in v3:
time: 114 us
  waiting for transfers between devices  63.4 us (56%)
  matrix products  25.1 us (22%)
  starting transfers between devices  16.4 us (14%)
  other arithmetic  4.8 us (4%)
  local copies, waits for them, and re-layouts  2.54 us (2%)
  between operations  1.71 us (2%)
    ppermute x6, waiting for transfers between devices, from_behind(): return lax.ppermute(block, axis, route)  63.4 us
    ppermute x6, starting transfers between devices, from_behind(): return lax.ppermute(block, axis, route)  16.4 us
    dot_general x3, matrix products, contract_rows(): lax.dot_general(left, right, (((0,), (0,)), ((), ())), preferred_element_...  10.5 us
    dot_general x6, matrix products, contract_cols(): lax.dot_general(left, right, (((1,), (1,)), ((), ())), preferred_element_...  6.57 us
    dot_general x2, matrix products, expert_up(): gate_pre = jnp.dot(rows_in, gate_w, preferred_element_type=jnp.float32)  3.98 us
    unnamed x11, local copies, waits for them, and re-layouts  2.44 us
  transfers between devices with their start and end apart: 6, of which 3 were waited for; matrix products, arithmetic and copies ran while one was open for 25% of the time, Pallas kernels for 0%

profile of v3, /device:TPU:17, one launch (start us, length us, event | category | flops | bytes accessed | tf_op | source)
XLA Modules:
  0.0 113.8 jit_solution(14890691990831303121)
XLA Ops:
  0.6 0.0 copy-start
  1.5 0.0 copy-start.4
  1.5 0.8 fusion.60
  2.3 4.6 %collective-permute-start.1 = (bf16[256]{0:T(256)(128)(2,1)S(1)}, bf16[256]{0:T(256)(128)(2,1)S(1)}, u32[]{:S(2)}, u32[]{:S(2)}) collective-permute-start(bf16[256]{0:T(256)(128)(2,1)S(1)} %get-tuple-element.49), channel_id=1, source_target_pairs={{1,0},{2,1},{3,2},{4,3},{5,4},{6,5},{7,6},{8,7},{9,8},{10,9},{11,1... | collective-permute-start | bytes 1544 | tf_op jit(solution)/shard_map/ppermute | solution.py:10
  6.9 2.4 %collective-permute-start.3 = (bf16[256,2048]{1,0:T(8,128)(2,1)}, bf16[256,2048]{1,0:T(8,128)(2,1)S(1)}, u32[]{:S(2)}, u32[]{:S(2)}) collective-permute-start(bf16[256,2048]{1,0:T(8,128)(2,1)} %param.9), channel_id=1, source_target_pairs={{1,0},{2,1},{3,2},{4,3},{5,4},{6,5},{7,6},{8,7},{9,8},{10,9},{11,1... | collective-permute-start | bytes 3145736 | tf_op jit(solution)/shard_map/ppermute | solution.py:10
  9.4 3.3 %collective-permute-start = (bf16[256,2048]{1,0:T(8,128)(2,1)}, bf16[256,2048]{1,0:T(8,128)(2,1)S(1)}, u32[]{:S(2)}, u32[]{:S(2)}) collective-permute-start(bf16[256,2048]{1,0:T(8,128)(2,1)} %param.7), channel_id=1, source_target_pairs={{1,0},{2,1},{3,2},{4,3},{5,4},{6,5},{7,6},{8,7},{9,8},{10,9},{11,1... | collective-permute-start | bytes 3145736 | tf_op jit(solution)/shard_map/ppermute | solution.py:10
  12.7 1.3 %constant_dynamic-update-slice_fusion.1 = bf16[512,2048]{1,0:T(8,128)(2,1)S(1)} fusion(bf16[256,2048]{1,0:T(8,128)(2,1)} %param.7), kind=kLoop, calls=%fused_computation.68 | loop fusion | bytes 2097152
  14.1 0.0 copy-done.4
  14.1 0.0 copy-start.2
  14.1 3.0 %fusion.20 = f32[256,768]{1,0:T(8,128)S(1)} fusion(bf16[256,2048]{1,0:T(8,128)(2,1)S(1)} %copy-done.4, bf16[1,2048,768]{2,1,0:T(8,128)(2,1)} %param.11), kind=kOutput, calls=%fused_computation.23 | convolution fusion | flops 805306368 | bytes 4980736 | tf_op jit(solution)/shard_map/dot_general | solution.py:26
  17.1 0.0 copy-done.2
  17.1 0.0 copy-start.3
  17.1 1.0 multiply_convert_fusion.6
  18.1 0.2 copy-done.3
  18.4 0.3 fusion.46
  18.7 0.0 copy-done
  18.7 1.0 multiply_convert_fusion
  19.7 1.2 %multiply_convert_fusion.4 = (bf16[256,768]{1,0:T(8,128)(2,1)S(1)}, bf16[256,768]{1,0:T(8,128)(2,1)S(1)}) fusion(f32[256,768]{1,0:T(8,128)S(1)} %fusion.20, f32[256,768]{1,0:T(8,128)S(1)} %get-tuple-element.28, bf16[256,2048]{1,0:T(8,128)(2,1)S(1)} %fusion.46, bf16[1,768,2048]{2,1,0:T(8,128)(2,1)S(1)} %copy-done), kind=kOutput, calls=%fused_computation.62 | convolution fusion | flops 807862272 | bytes 6553600 | tf_op jit(solution)/shard_map/dot_general | solution.py:20
  20.9 0.3 fusion.40
  21.2 0.0 copy-start.1
  21.2 1.0 fusion.10
  22.3 0.9 copy-done.1
  23.1 1.0 fusion.36
  24.2 0.0 collective-permute-done.1
  24.2 32.3 %collective-permute-done = bf16[256,2048]{1,0:T(8,128)(2,1)S(1)} collective-permute-done((bf16[256,2048]{1,0:T(8,128)(2,1)}, bf16[256,2048]{1,0:T(8,128)(2,1)S(1)}, u32[]{:S(2)}, u32[]{:S(2)}) %collective-permute-start) | collective-permute-done | bytes 1048608 | tf_op jit(solution)/shard_map/ppermute | solution.py:10
  56.5 1.0 fusion.22
  57.5 1.0 multiply_convert_fusion.7
  58.5 1.0 multiply_convert_fusion.1
  59.5 0.0 collective-permute-done.3
  59.5 0.5 fusion.42
  60.0 1.9 %collective-permute-start.4 = (bf16[256]{0:T(256)(128)(2,1)S(1)}, bf16[256]{0:T(256)(128)(2,1)S(1)}, u32[]{:S(2)}, u32[]{:S(2)}) collective-permute-start(bf16[256]{0:T(256)(128)(2,1)S(1)} %get-tuple-element.47), channel_id=1, source_target_pairs={{0,1},{1,2},{2,3},{3,4},{4,5},{5,6},{6,7},{7,8},{8,9},{9,10},{10,1... | collective-permute-start | bytes 1544 | tf_op jit(solution)/shard_map/ppermute | solution.py:10
  62.0 1.9 %collective-permute-start.2 = (bf16[256,2048]{1,0:T(8,128)(2,1)S(1)}, bf16[256,2048]{1,0:T(8,128)(2,1)S(1)}, u32[]{:S(2)}, u32[]{:S(2)}) collective-permute-start(bf16[256,2048]{1,0:T(8,128)(2,1)S(1)} %get-tuple-element.25), channel_id=1, source_target_pairs={{0,1},{1,2},{2,3},{3,4},{4,5},{5,6},{6,7},{7,8},{8,9},{9,10},{10,1... | collective-permute-start | bytes 3145736 | tf_op jit(solution)/shard_map/ppermute | solution.py:10
  63.9 1.2 %multiply_convert_fusion.2 = (bf16[256,768]{1,0:T(8,128)(2,1)S(1)}, bf16[256,768]{1,0:T(8,128)(2,1)S(1)}) fusion(f32[256,768]{1,0:T(8,128)S(1)} %fusion.22, f32[256,768]{1,0:T(8,128)S(1)} %get-tuple-element.34, bf16[256,2048]{1,0:T(8,128)(2,1)S(1)} %get-tuple-element.46, bf16[1,768,2048]{2,1,0:T(8,128)(2,1)S(1)} %copy-done), kind=kOutput, calls=%fused_computation.59 | convolution fusion | flops 807862272 | bytes 6553600 | tf_op jit(solution)/shard_map/dot_general | solution.py:20
  65.1 1.0 fusion.8
  66.2 1.1 fusion.33
  67.2 2.1 %collective-permute-start.5 = (bf16[256,2048]{1,0:T(8,128)(2,1)S(1)}, bf16[256,2048]{1,0:T(8,128)(2,1)S(1)}, u32[]{:S(2)}, u32[]{:S(2)}) collective-permute-start(bf16[256,2048]{1,0:T(8,128)(2,1)S(1)} %fusion.33), channel_id=1, source_target_pairs={{0,1},{1,2},{2,3},{3,4},{4,5},{5,6},{6,7},{7,8},{8,9},{9,10},{10,1... | collective-permute-start | bytes 3145736 | tf_op jit(solution)/shard_map/ppermute | solution.py:10
  69.3 0.1 constant_dynamic-update-slice_fusion
  69.4 3.5 %fusion.24 = bf16[1,2048,768]{2,1,0:T(8,128)(2,1)} fusion(bf16[512,2048]{1,0:T(8,128)(2,1)S(1)} %constant_dynamic-update-slice_fusion, bf16[256,768]{1,0:T(8,128)(2,1)S(1)} %get-tuple-element.39, bf16[256,768]{1,0:T(8,128)(2,1)S(1)} %get-tuple-element.38), kind=kOutput, calls=%fused_computation.27 | convolution fusion | flops 1613758464 | bytes 6029312 | tf_op jit(solution)/shard_map/dot_general | solution.py:14
  73.0 3.5 %fusion.25 = bf16[1,2048,768]{2,1,0:T(8,128)(2,1)} fusion(bf16[512,2048]{1,0:T(8,128)(2,1)S(1)} %constant_dynamic-update-slice_fusion, bf16[256,768]{1,0:T(8,128)(2,1)S(1)} %get-tuple-element.41, bf16[256,768]{1,0:T(8,128)(2,1)S(1)} %get-tuple-element.40), kind=kOutput, calls=%fused_computation.28 | convolution fusion | flops 1613758464 | bytes 6029312 | tf_op jit(solution)/shard_map/dot_general | solution.py:14
  76.5 3.5 %fusion.26 = bf16[1,768,2048]{2,1,0:T(8,128)(2,1)} fusion(bf16[256,2048]{1,0:T(8,128)(2,1)S(1)} %get-tuple-element.46, bf16[256,2048]{1,0:T(8,128)(2,1)S(1)} %fusion.46, bf16[256,768]{1,0:T(8,128)(2,1)S(1)} %get-tuple-element.24, bf16[256,768]{1,0:T(8,128)(2,1)S(1)} %get-tuple-element.26), kind=kOutput, calls=%fused_computation.29 | convolution fusion | flops 1617952768 | bytes 6029312 | tf_op jit(solution)/shard_map/dot_general | solution.py:14
  80.0 0.0 collective-permute-done.4
  80.0 0.5 convert_select_fusion
  80.5 21.0 %collective-permute-done.2 = bf16[256,2048]{1,0:T(8,128)(2,1)S(1)} collective-permute-done((bf16[256,2048]{1,0:T(8,128)(2,1)S(1)}, bf16[256,2048]{1,0:T(8,128)(2,1)S(1)}, u32[]{:S(2)}, u32[]{:S(2)}) %collective-permute-start.2) | collective-permute-done | bytes 1048608 | tf_op jit(solution)/shard_map/ppermute | solution.py:10
  101.5 1.1 %broadcast_select_fusion.1 = bf16[256,2048]{1,0:T(8,128)(2,1)} fusion(bf16[256,2048]{1,0:T(8,128)(2,1)S(1)} %collective-permute-done.2, bf16[256,2048]{1,0:T(8,128)(2,1)S(1)} %get-tuple-element.27, pred[256]{0:T(512)(128)(4,1)S(1)} %iota_compare_fusion), kind=kLoop, calls=%fused_computation.49 | loop fusion | flops 524288 | bytes 3145984 | tf_op jit(solution)/shard_map/jit(_where)/select_n | solution.py:102
  102.6 10.1 %collective-permute-done.5 = bf16[256,2048]{1,0:T(8,128)(2,1)S(1)} collective-permute-done((bf16[256,2048]{1,0:T(8,128)(2,1)S(1)}, bf16[256,2048]{1,0:T(8,128)(2,1)S(1)}, u32[]{:S(2)}, u32[]{:S(2)}) %collective-permute-start.5) | collective-permute-done | bytes 1048608 | tf_op jit(solution)/shard_map/ppermute | solution.py:10
  112.7 1.1 %broadcast_select_fusion = bf16[256,2048]{1,0:T(8,128)(2,1)} fusion(bf16[256,2048]{1,0:T(8,128)(2,1)S(1)} %collective-permute-done.5, bf16[256,2048]{1,0:T(8,128)(2,1)S(1)} %fusion.36, pred[256]{0:T(512)(128)(4,1)S(1)} %iota_compare_fusion), kind=kLoop, calls=%fused_computation.48 | loop fusion | flops 524288 | bytes 3145984 | tf_op jit(solution)/shard_map/jit(_where)/select_n | solution.py:105
  (3 shorter events, 0.0 us)
Async XLA Ops:
  0.6 18.0 %copy-start = (bf16[1,768,2048]{2,1,0:T(8,128)(2,1)S(1)}, bf16[1,768,2048]{2,1,0:T(8,128)(2,1)}, u32[]{:S(2)}) copy-start(bf16[1,768,2048]{2,1,0:T(8,128)(2,1)} %param.13) | copy-start | bytes 9437188
  1.5 12.6 %copy-start.4 = (bf16[256,2048]{1,0:T(8,128)(2,1)S(1)}, bf16[256,2048]{1,0:T(8,128)(2,1)}, u32[]{:S(2)}) copy-start(bf16[256,2048]{1,0:T(8,128)(2,1)} %param.7) | copy-start | bytes 3145732
  2.3 21.9 %collective-permute-start.1 = (bf16[256]{0:T(256)(128)(2,1)S(1)}, bf16[256]{0:T(256)(128)(2,1)S(1)}, u32[]{:S(2)}, u32[]{:S(2)}) collective-permute-start(bf16[256]{0:T(256)(128)(2,1)S(1)} %get-tuple-element.49), channel_id=1, source_target_pairs={{1,0},{2,1},{3,2},{4,3},{5,4},{6,5},{7,6},{8,7},{9,8},{10,9},{11,1... | collective-permute-start | bytes 1544 | tf_op jit(solution)/shard_map/ppermute | solution.py:10
  6.9 52.6 %collective-permute-start.3 = (bf16[256,2048]{1,0:T(8,128)(2,1)}, bf16[256,2048]{1,0:T(8,128)(2,1)S(1)}, u32[]{:S(2)}, u32[]{:S(2)}) collective-permute-start(bf16[256,2048]{1,0:T(8,128)(2,1)} %param.9), channel_id=1, source_target_pairs={{1,0},{2,1},{3,2},{4,3},{5,4},{6,5},{7,6},{8,7},{9,8},{10,9},{11,1... | collective-permute-start | bytes 3145736 | tf_op jit(solution)/shard_map/ppermute | solution.py:10
  9.4 47.1 %collective-permute-start = (bf16[256,2048]{1,0:T(8,128)(2,1)}, bf16[256,2048]{1,0:T(8,128)(2,1)S(1)}, u32[]{:S(2)}, u32[]{:S(2)}) collective-permute-start(bf16[256,2048]{1,0:T(8,128)(2,1)} %param.7), channel_id=1, source_target_pairs={{1,0},{2,1},{3,2},{4,3},{5,4},{6,5},{7,6},{8,7},{9,8},{10,9},{11,1... | collective-permute-start | bytes 3145736 | tf_op jit(solution)/shard_map/ppermute | solution.py:10
  14.1 3.0 %copy-start.2 = (bf16[1,2048,768]{2,1,0:T(8,128)(2,1)S(1)}, bf16[1,2048,768]{2,1,0:T(8,128)(2,1)}, u32[]{:S(2)}) copy-start(bf16[1,2048,768]{2,1,0:T(8,128)(2,1)} %param.12) | copy-start | bytes 9437188
  17.1 1.2 %copy-start.3 = (bf16[256,2048]{1,0:T(8,128)(2,1)S(1)}, bf16[256,2048]{1,0:T(8,128)(2,1)}, u32[]{:S(2)}) copy-start(bf16[256,2048]{1,0:T(8,128)(2,1)} %param.9) | copy-start | bytes 3145732
  21.2 1.9 %copy-start.1 = (bf16[1,2048,768]{2,1,0:T(8,128)(2,1)S(1)}, bf16[1,2048,768]{2,1,0:T(8,128)(2,1)}, u32[]{:S(2)}) copy-start(bf16[1,2048,768]{2,1,0:T(8,128)(2,1)} %param.11) | copy-start | bytes 9437188
  60.0 19.9 %collective-permute-start.4 = (bf16[256]{0:T(256)(128)(2,1)S(1)}, bf16[256]{0:T(256)(128)(2,1)S(1)}, u32[]{:S(2)}, u32[]{:S(2)}) collective-permute-start(bf16[256]{0:T(256)(128)(2,1)S(1)} %get-tuple-element.47), channel_id=1, source_target_pairs={{0,1},{1,2},{2,3},{3,4},{4,5},{5,6},{6,7},{7,8},{8,9},{9,10},{10,1... | collective-permute-start | bytes 1544 | tf_op jit(solution)/shard_map/ppermute | solution.py:10
  62.0 39.5 %collective-permute-start.2 = (bf16[256,2048]{1,0:T(8,128)(2,1)S(1)}, bf16[256,2048]{1,0:T(8,128)(2,1)S(1)}, u32[]{:S(2)}, u32[]{:S(2)}) collective-permute-start(bf16[256,2048]{1,0:T(8,128)(2,1)S(1)} %get-tuple-element.25), channel_id=1, source_target_pairs={{0,1},{1,2},{2,3},{3,4},{4,5},{5,6},{6,7},{7,8},{8,9},{9,10},{10,1... | collective-permute-start | bytes 3145736 | tf_op jit(solution)/shard_map/ppermute | solution.py:10
  67.2 45.5 %collective-permute-start.5 = (bf16[256,2048]{1,0:T(8,128)(2,1)S(1)}, bf16[256,2048]{1,0:T(8,128)(2,1)S(1)}, u32[]{:S(2)}, u32[]{:S(2)}) collective-permute-start(bf16[256,2048]{1,0:T(8,128)(2,1)S(1)} %fusion.33), channel_id=1, source_target_pairs={{0,1},{1,2},{2,3},{3,4},{4,5},{5,6},{6,7},{7,8},{8,9},{9,10},{10,1... | collective-permute-start | bytes 3145736 | tf_op jit(solution)/shard_map/ppermute | solution.py:10

commit v4 on v3

--- a/solution.py
+++ b/solution.py
@@ -87,7 +87,9 @@
         next_out_grad, next_pre, gate_w, up_w, down_w
     )
     back_comb_grad = from_behind(next_comb_grad, axes, 1)
-    back_in_grad = from_behind(next_in_grad, axes, 1)
+    cut = count_rows - count_rows // TAIL_SHARE
+    back_head = from_behind(next_in_grad[:cut], axes, 1)
+    back_tail = from_behind(next_in_grad[cut:], axes, 1)
 
     rows_all = jnp.concatenate([sorted_rows, next_rows], axis=0)
     hidden_all = jnp.concatenate([own_pre[2], next_pre[2]], axis=0)
@@ -102,8 +104,14 @@
     mixed = jnp.where(lead_mask[:, None], back_mixed, own_mixed)
     mixed, own_in_grad = lax.optimization_barrier((mixed, own_in_grad))
     row = lax.broadcasted_iota(jnp.int32, own_in_grad.shape, 0)
-    in_grad = jnp.where(row < lead_count, back_in_grad, own_in_grad)
+    joined = jnp.where(row[:cut] < lead_count, back_head, own_in_grad[:cut])
+    in_grad = lax.optimization_barrier(lax.dynamic_update_slice(own_in_grad, joined, (0, 0)))
+    joined = jnp.where(row[cut:] < lead_count, back_tail, in_grad[cut:])
+    in_grad = lax.dynamic_update_slice(in_grad, joined, (cut, 0))
     return (mixed, comb_grad, in_grad, grad_gate, grad_up, grad_down)
+
+
+TAIL_SHARE = 4
 
 
 def solution(mesh):

time: 114 us -> 114 us (level)
  waiting for transfers between devices: 63.4 us -> 55.7 us
  starting transfers between devices: 16.4 us -> 23.5 us
    ppermute x6 -> x7, waiting for transfers between devices: 63.4 us -> 55.7 us  [from_behind(): return lax.ppermute(block, axis, route)]
    ppermute x6 -> x7, starting transfers between devices: 16.4 us -> 23.5 us  [from_behind(): return lax.ppermute(block, axis, route)]
    select_n x1 -> x0, other arithmetic: 1.14 us -> none  [device_step(): in_grad = jnp.where(row < lead_count, back_in_grad, own_in_grad)]
    unnamed x11 -> x13, local copies, waits for them, and re-layouts: 2.44 us -> 3.39 us
  transfers between devices with their start and end apart: 6 -> 7, of which waited for: 3 -> 4; matrix products, arithmetic and copies ran while one was open for 25% -> 26% of each run, Pallas kernels for 0% -> 0%
where the time goes in v4:
time: 114 us
  waiting for transfers between devices  55.7 us (49%)
  matrix products  25.1 us (22%)
  starting transfers between devices  23.5 us (21%)
  other arithmetic  4.12 us (4%)
  local copies, waits for them, and re-layouts  3.58 us (3%)
  between operations  1.76 us (2%)
    ppermute x7, waiting for transfers between devices, from_behind(): return lax.ppermute(block, axis, route)  55.7 us
    ppermute x7, starting transfers between devices, from_behind(): return lax.ppermute(block, axis, route)  23.5 us
    dot_general x3, matrix products, contract_rows(): lax.dot_general(left, right, (((0,), (0,)), ((), ())), preferred_element_...  10.5 us
    dot_general x6, matrix products, contract_cols(): lax.dot_general(left, right, (((1,), (1,)), ((), ())), preferred_element_...  6.6 us
    dot_general x2, matrix products, expert_up(): gate_pre = jnp.dot(rows_in, gate_w, preferred_element_type=jnp.float32)  3.98 us
    unnamed x13, local copies, waits for them, and re-layouts  3.39 us
  transfers between devices with their start and end apart: 7, of which 4 were waited for; matrix products, arithmetic and copies ran while one was open for 26% of the time, Pallas kernels for 0%

profile of v4, /device:TPU:17, one launch (start us, length us, event | category | flops | bytes accessed | tf_op | source)
XLA Modules:
  0.0 113.8 jit_solution(15049441251809730664)
XLA Ops:
  0.6 0.0 copy-start
  1.5 0.0 copy-start.5
  1.5 0.8 fusion.64
  2.3 4.6 %collective-permute-start.1 = (bf16[256]{0:T(256)(128)(2,1)S(1)}, bf16[256]{0:T(256)(128)(2,1)S(1)}, u32[]{:S(2)}, u32[]{:S(2)}) collective-permute-start(bf16[256]{0:T(256)(128)(2,1)S(1)} %get-tuple-element.49), channel_id=1, source_target_pairs={{1,0},{2,1},{3,2},{4,3},{5,4},{6,5},{7,6},{8,7},{9,8},{10,9},{11,1... | collective-permute-start | bytes 1544 | tf_op jit(solution)/shard_map/ppermute | solution.py:10
  6.9 2.4 %collective-permute-start.3 = (bf16[256,2048]{1,0:T(8,128)(2,1)}, bf16[256,2048]{1,0:T(8,128)(2,1)S(1)}, u32[]{:S(2)}, u32[]{:S(2)}) collective-permute-start(bf16[256,2048]{1,0:T(8,128)(2,1)} %param.9), channel_id=1, source_target_pairs={{1,0},{2,1},{3,2},{4,3},{5,4},{6,5},{7,6},{8,7},{9,8},{10,9},{11,1... | collective-permute-start | bytes 3145736 | tf_op jit(solution)/shard_map/ppermute | solution.py:10
  9.4 3.3 %collective-permute-start = (bf16[256,2048]{1,0:T(8,128)(2,1)}, bf16[256,2048]{1,0:T(8,128)(2,1)S(1)}, u32[]{:S(2)}, u32[]{:S(2)}) collective-permute-start(bf16[256,2048]{1,0:T(8,128)(2,1)} %param.7), channel_id=1, source_target_pairs={{1,0},{2,1},{3,2},{4,3},{5,4},{6,5},{7,6},{8,7},{9,8},{10,9},{11,1... | collective-permute-start | bytes 3145736 | tf_op jit(solution)/shard_map/ppermute | solution.py:10
  12.7 1.3 %constant_dynamic-update-slice_fusion.1 = bf16[512,2048]{1,0:T(8,128)(2,1)S(1)} fusion(bf16[256,2048]{1,0:T(8,128)(2,1)} %param.7), kind=kLoop, calls=%fused_computation.73 | loop fusion | bytes 2097152
  14.1 0.0 copy-start.2
  14.1 3.0 %fusion.20 = f32[256,768]{1,0:T(8,128)S(1)} fusion(bf16[256,2048]{1,0:T(8,128)(2,1)S(1)} %copy-done.5, bf16[1,2048,768]{2,1,0:T(8,128)(2,1)} %param.11), kind=kOutput, calls=%fused_computation.23 | convolution fusion | flops 805306368 | bytes 4980736 | tf_op jit(solution)/shard_map/dot_general | solution.py:26
  17.1 0.0 copy-start.4
  17.1 1.0 multiply_convert_fusion.6
  18.2 0.2 copy-done.4
  18.4 0.3 fusion.47
  18.7 1.0 multiply_convert_fusion
  19.7 1.2 %multiply_convert_fusion.4 = (bf16[256,768]{1,0:T(8,128)(2,1)S(1)}, bf16[256,768]{1,0:T(8,128)(2,1)S(1)}) fusion(f32[256,768]{1,0:T(8,128)S(1)} %fusion.20, f32[256,768]{1,0:T(8,128)S(1)} %get-tuple-element.28, bf16[256,2048]{1,0:T(8,128)(2,1)S(1)} %fusion.47, bf16[1,768,2048]{2,1,0:T(8,128)(2,1)S(1)} %copy-done), kind=kOutput, calls=%fused_computation.64 | convolution fusion | flops 807862272 | bytes 6553600 | tf_op jit(solution)/shard_map/dot_general | solution.py:20
  20.9 0.3 fusion.40
  21.2 1.0 fusion.10
  22.2 0.9 copy-done.1
  23.1 1.1 fusion.36
  24.2 0.0 collective-permute-done.1
  24.2 32.3 %collective-permute-done = bf16[256,2048]{1,0:T(8,128)(2,1)S(1)} collective-permute-done((bf16[256,2048]{1,0:T(8,128)(2,1)}, bf16[256,2048]{1,0:T(8,128)(2,1)S(1)}, u32[]{:S(2)}, u32[]{:S(2)}) %collective-permute-start) | collective-permute-done | bytes 1048608 | tf_op jit(solution)/shard_map/ppermute | solution.py:10
  56.5 1.0 fusion.22
  57.5 1.0 multiply_convert_fusion.7
  58.5 1.0 multiply_convert_fusion.1
  59.5 0.0 collective-permute-done.3
  59.5 0.5 fusion.42
  60.0 1.9 %collective-permute-start.4 = (bf16[256]{0:T(256)(128)(2,1)S(1)}, bf16[256]{0:T(256)(128)(2,1)S(1)}, u32[]{:S(2)}, u32[]{:S(2)}) collective-permute-start(bf16[256]{0:T(256)(128)(2,1)S(1)} %get-tuple-element.47), channel_id=1, source_target_pairs={{0,1},{1,2},{2,3},{3,4},{4,5},{5,6},{6,7},{7,8},{8,9},{9,10},{10,1... | collective-permute-start | bytes 1544 | tf_op jit(solution)/shard_map/ppermute | solution.py:10
  62.0 1.9 %collective-permute-start.2 = (bf16[256,2048]{1,0:T(8,128)(2,1)S(1)}, bf16[256,2048]{1,0:T(8,128)(2,1)S(1)}, u32[]{:S(2)}, u32[]{:S(2)}) collective-permute-start(bf16[256,2048]{1,0:T(8,128)(2,1)S(1)} %get-tuple-element.25), channel_id=1, source_target_pairs={{0,1},{1,2},{2,3},{3,4},{4,5},{5,6},{6,7},{7,8},{8,9},{9,10},{10,1... | collective-permute-start | bytes 3145736 | tf_op jit(solution)/shard_map/ppermute | solution.py:10
  63.9 1.2 %multiply_convert_fusion.2 = (bf16[256,768]{1,0:T(8,128)(2,1)S(1)}, bf16[256,768]{1,0:T(8,128)(2,1)S(1)}) fusion(f32[256,768]{1,0:T(8,128)S(1)} %fusion.22, f32[256,768]{1,0:T(8,128)S(1)} %get-tuple-element.35, bf16[256,2048]{1,0:T(8,128)(2,1)S(1)} %get-tuple-element.46, bf16[1,768,2048]{2,1,0:T(8,128)(2,1)S(1)} %copy-done), kind=kOutput, calls=%fused_computation.61 | convolution fusion | flops 807862272 | bytes 6553600 | tf_op jit(solution)/shard_map/dot_general | solution.py:20
  65.1 1.0 fusion.8
  66.2 1.1 fusion.33
  67.2 0.1 slice.19
  67.3 2.1 %collective-permute-start.5 = (bf16[192,2048]{1,0:T(8,128)(2,1)S(1)}, bf16[192,2048]{1,0:T(8,128)(2,1)S(1)}, u32[]{:S(2)}, u32[]{:S(2)}) collective-permute-start(bf16[192,2048]{1,0:T(8,128)(2,1)S(1)} %slice.19), channel_id=1, source_target_pairs={{0,1},{1,2},{2,3},{3,4},{4,5},{5,6},{6,7},{7,8},{8,9},{9,10},{10,1... | collective-permute-start | bytes 2359304 | tf_op jit(solution)/shard_map/ppermute | solution.py:10
  69.4 0.1 constant_dynamic-update-slice_fusion
  69.5 3.5 %fusion.24 = bf16[1,2048,768]{2,1,0:T(8,128)(2,1)} fusion(bf16[512,2048]{1,0:T(8,128)(2,1)S(1)} %constant_dynamic-update-slice_fusion, bf16[256,768]{1,0:T(8,128)(2,1)S(1)} %get-tuple-element.39, bf16[256,768]{1,0:T(8,128)(2,1)S(1)} %get-tuple-element.38), kind=kOutput, calls=%fused_computation.27 | convolution fusion | flops 1613758464 | bytes 6029312 | tf_op jit(solution)/shard_map/dot_general | solution.py:14
  73.0 3.5 %fusion.25 = bf16[1,2048,768]{2,1,0:T(8,128)(2,1)} fusion(bf16[512,2048]{1,0:T(8,128)(2,1)S(1)} %constant_dynamic-update-slice_fusion, bf16[256,768]{1,0:T(8,128)(2,1)S(1)} %get-tuple-element.41, bf16[256,768]{1,0:T(8,128)(2,1)S(1)} %get-tuple-element.40), kind=kOutput, calls=%fused_computation.28 | convolution fusion | flops 1613758464 | bytes 6029312 | tf_op jit(solution)/shard_map/dot_general | solution.py:14
  76.6 3.5 %fusion.26 = bf16[1,768,2048]{2,1,0:T(8,128)(2,1)} fusion(bf16[256,2048]{1,0:T(8,128)(2,1)S(1)} %get-tuple-element.46, bf16[256,2048]{1,0:T(8,128)(2,1)S(1)} %fusion.47, bf16[256,768]{1,0:T(8,128)(2,1)S(1)} %get-tuple-element.24, bf16[256,768]{1,0:T(8,128)(2,1)S(1)} %get-tuple-element.26), kind=kOutput, calls=%fused_computation.29 | convolution fusion | flops 1617952768 | bytes 6029312 | tf_op jit(solution)/shard_map/dot_general | solution.py:14
  80.1 7.2 %collective-permute-start.6 = (bf16[64,2048]{1,0:T(8,128)(2,1)S(1)}, bf16[64,2048]{1,0:T(8,128)(2,1)S(1)}, u32[]{:S(2)}, u32[]{:S(2)}) collective-permute-start(bf16[64,2048]{1,0:T(8,128)(2,1)S(1)} %slice.22), channel_id=1, source_target_pairs={{0,1},{1,2},{2,3},{3,4},{4,5},{5,6},{6,7},{7,8},{8,9},{9,10},{10,1... | collective-permute-start | bytes 786440 | tf_op jit(solution)/shard_map/ppermute | solution.py:10
  87.3 0.0 collective-permute-done.4
  87.3 0.5 convert_select_fusion
  87.8 13.7 %collective-permute-done.2 = bf16[256,2048]{1,0:T(8,128)(2,1)S(1)} collective-permute-done((bf16[256,2048]{1,0:T(8,128)(2,1)S(1)}, bf16[256,2048]{1,0:T(8,128)(2,1)S(1)}, u32[]{:S(2)}, u32[]{:S(2)}) %collective-permute-start.2) | collective-permute-done | bytes 1048608 | tf_op jit(solution)/shard_map/ppermute | solution.py:10
  101.5 1.1 %broadcast_select_fusion = bf16[256,2048]{1,0:T(8,128)(2,1)} fusion(bf16[256,2048]{1,0:T(8,128)(2,1)S(1)} %collective-permute-done.2, bf16[256,2048]{1,0:T(8,128)(2,1)S(1)} %get-tuple-element.27, pred[256]{0:T(512)(128)(4,1)S(1)} %iota_compare_fusion), kind=kLoop, calls=%fused_computation.50 | loop fusion | flops 524288 | bytes 3145984 | tf_op jit(solution)/shard_map/jit(_where)/select_n | solution.py:104
  102.6 7.3 %collective-permute-done.5 = bf16[192,2048]{1,0:T(8,128)(2,1)S(1)} collective-permute-done((bf16[192,2048]{1,0:T(8,128)(2,1)S(1)}, bf16[192,2048]{1,0:T(8,128)(2,1)S(1)}, u32[]{:S(2)}, u32[]{:S(2)}) %collective-permute-start.5) | collective-permute-done | bytes 786464 | tf_op jit(solution)/shard_map/ppermute | solution.py:10
  109.9 0.4 fusion.48
  110.3 2.4 %collective-permute-done.6 = bf16[64,2048]{1,0:T(8,128)(2,1)S(1)} collective-permute-done((bf16[64,2048]{1,0:T(8,128)(2,1)S(1)}, bf16[64,2048]{1,0:T(8,128)(2,1)S(1)}, u32[]{:S(2)}, u32[]{:S(2)}) %collective-permute-start.6) | collective-permute-done | bytes 262176 | tf_op jit(solution)/shard_map/ppermute | solution.py:10
  112.7 0.1 fusion.59
  112.8 0.0 copy-start.3
  112.8 1.0 copy-done.3
  (8 shorter events, 0.0 us)
Async XLA Ops:
  0.6 18.0 %copy-start = (bf16[1,768,2048]{2,1,0:T(8,128)(2,1)S(1)}, bf16[1,768,2048]{2,1,0:T(8,128)(2,1)}, u32[]{:S(2)}) copy-start(bf16[1,768,2048]{2,1,0:T(8,128)(2,1)} %param.13) | copy-start | bytes 9437188
  1.5 12.6 %copy-start.5 = (bf16[256,2048]{1,0:T(8,128)(2,1)S(1)}, bf16[256,2048]{1,0:T(8,128)(2,1)}, u32[]{:S(2)}) copy-start(bf16[256,2048]{1,0:T(8,128)(2,1)} %param.7) | copy-start | bytes 3145732
  2.3 21.9 %collective-permute-start.1 = (bf16[256]{0:T(256)(128)(2,1)S(1)}, bf16[256]{0:T(256)(128)(2,1)S(1)}, u32[]{:S(2)}, u32[]{:S(2)}) collective-permute-start(bf16[256]{0:T(256)(128)(2,1)S(1)} %get-tuple-element.49), channel_id=1, source_target_pairs={{1,0},{2,1},{3,2},{4,3},{5,4},{6,5},{7,6},{8,7},{9,8},{10,9},{11,1... | collective-permute-start | bytes 1544 | tf_op jit(solution)/shard_map/ppermute | solution.py:10
  6.9 52.6 %collective-permute-start.3 = (bf16[256,2048]{1,0:T(8,128)(2,1)}, bf16[256,2048]{1,0:T(8,128)(2,1)S(1)}, u32[]{:S(2)}, u32[]{:S(2)}) collective-permute-start(bf16[256,2048]{1,0:T(8,128)(2,1)} %param.9), channel_id=1, source_target_pairs={{1,0},{2,1},{3,2},{4,3},{5,4},{6,5},{7,6},{8,7},{9,8},{10,9},{11,1... | collective-permute-start | bytes 3145736 | tf_op jit(solution)/shard_map/ppermute | solution.py:10
  9.4 47.1 %collective-permute-start = (bf16[256,2048]{1,0:T(8,128)(2,1)}, bf16[256,2048]{1,0:T(8,128)(2,1)S(1)}, u32[]{:S(2)}, u32[]{:S(2)}) collective-permute-start(bf16[256,2048]{1,0:T(8,128)(2,1)} %param.7), channel_id=1, source_target_pairs={{1,0},{2,1},{3,2},{4,3},{5,4},{6,5},{7,6},{8,7},{9,8},{10,9},{11,1... | collective-permute-start | bytes 3145736 | tf_op jit(solution)/shard_map/ppermute | solution.py:10
  14.1 3.0 %copy-start.2 = (bf16[1,2048,768]{2,1,0:T(8,128)(2,1)S(1)}, bf16[1,2048,768]{2,1,0:T(8,128)(2,1)}, u32[]{:S(2)}) copy-start(bf16[1,2048,768]{2,1,0:T(8,128)(2,1)} %param.12) | copy-start | bytes 9437188
  17.1 1.2 %copy-start.4 = (bf16[256,2048]{1,0:T(8,128)(2,1)S(1)}, bf16[256,2048]{1,0:T(8,128)(2,1)}, u32[]{:S(2)}) copy-start(bf16[256,2048]{1,0:T(8,128)(2,1)} %param.9) | copy-start | bytes 3145732
  21.2 1.9 %copy-start.1 = (bf16[1,2048,768]{2,1,0:T(8,128)(2,1)S(1)}, bf16[1,2048,768]{2,1,0:T(8,128)(2,1)}, u32[]{:S(2)}) copy-start(bf16[1,2048,768]{2,1,0:T(8,128)(2,1)} %param.11) | copy-start | bytes 9437188
  60.0 27.2 %collective-permute-start.4 = (bf16[256]{0:T(256)(128)(2,1)S(1)}, bf16[256]{0:T(256)(128)(2,1)S(1)}, u32[]{:S(2)}, u32[]{:S(2)}) collective-permute-start(bf16[256]{0:T(256)(128)(2,1)S(1)} %get-tuple-element.47), channel_id=1, source_target_pairs={{0,1},{1,2},{2,3},{3,4},{4,5},{5,6},{6,7},{7,8},{8,9},{9,10},{10,1... | collective-permute-start | bytes 1544 | tf_op jit(solution)/shard_map/ppermute | solution.py:10
  62.0 39.5 %collective-permute-start.2 = (bf16[256,2048]{1,0:T(8,128)(2,1)S(1)}, bf16[256,2048]{1,0:T(8,128)(2,1)S(1)}, u32[]{:S(2)}, u32[]{:S(2)}) collective-permute-start(bf16[256,2048]{1,0:T(8,128)(2,1)S(1)} %get-tuple-element.25), channel_id=1, source_target_pairs={{0,1},{1,2},{2,3},{3,4},{4,5},{5,6},{6,7},{7,8},{8,9},{9,10},{10,1... | collective-permute-start | bytes 3145736 | tf_op jit(solution)/shard_map/ppermute | solution.py:10
  67.3 42.6 %collective-permute-start.5 = (bf16[192,2048]{1,0:T(8,128)(2,1)S(1)}, bf16[192,2048]{1,0:T(8,128)(2,1)S(1)}, u32[]{:S(2)}, u32[]{:S(2)}) collective-permute-start(bf16[192,2048]{1,0:T(8,128)(2,1)S(1)} %slice.19), channel_id=1, source_target_pairs={{0,1},{1,2},{2,3},{3,4},{4,5},{5,6},{6,7},{7,8},{8,9},{9,10},{10,1... | collective-permute-start | bytes 2359304 | tf_op jit(solution)/shard_map/ppermute | solution.py:10
  80.1 32.6 %collective-permute-start.6 = (bf16[64,2048]{1,0:T(8,128)(2,1)S(1)}, bf16[64,2048]{1,0:T(8,128)(2,1)S(1)}, u32[]{:S(2)}, u32[]{:S(2)}) collective-permute-start(bf16[64,2048]{1,0:T(8,128)(2,1)S(1)} %slice.22), channel_id=1, source_target_pairs={{0,1},{1,2},{2,3},{3,4},{4,5},{5,6},{6,7},{7,8},{8,9},{9,10},{10,1... | collective-permute-start | bytes 786440 | tf_op jit(solution)/shard_map/ppermute | solution.py:10
  112.8 1.0 copy-start.3
